TPU v7x, 256 devices: a whole 4x4x8 slice. The times are simulated.
256 devices in a mesh: section: 16 (over z, x_hi), dp: 16 (over y, x_lo, core).
Axes of the slice: x: 4 (x_hi: 2, x_lo: 2; x = x_hi * 2 + x_lo), y: 4, z: 8, core: 2. Of those that a mesh axis runs over, the one named last changes fastest.
Arguments:
- clip_pool: bfloat16 [64, 3, 4, 2, 640], P('dp'), may hold values from -6 to 6
- sample_ids: int32 [128], P('dp'), may hold values from 0 to 3
- timesteps: int32 [128], P('dp'), may hold values from 0 to 999
- noise_draw: bfloat16 [128, 3, 4, 2, 640], P('dp'), may hold values from -6 to 6
- keep_lists: int32 [128, 32], P('dp'), may hold values 0 or 1
- enc_weight: bfloat16 [16, 5760, 640], P('section'), may hold values from -0.078125 to 0.078125
- enc_gain: float32 [16, 640], P('section'), may hold values from 0.1 to 1.9
- dec_weight: bfloat16 [16, 1920, 640], P('section'), may hold values from -0.125 to 0.125
- dec_gain: float32 [16, 640], P('section'), may hold values from 0.1 to 1.9
Outputs:
- enc_weight_grad: float32 [16, 5760, 640], P('section', 'dp')
- enc_gain_grad: float32 [16, 640], P('section', 'dp')
- dec_weight_grad: float32 [16, 1920, 640], P('section', 'dp')
- dec_gain_grad: float32 [16, 640], P('section', 'dp')
All inputs are finite; a program needn't handle non-finite values. No bound on the sum of `keep_lists` on one device may be relied on, other than what follows from the above.
Results may differ from a plain program's by a relative error of at most 0.025.
Values may be sent and summed in bfloat16 or wider, within the bound.
A program may use at most 64 MiB of HBM per device.

v0:
```python
import math

import jax
import jax.numpy as jnp
from jax import lax
from jax.sharding import PartitionSpec as P

GROUPS = 32


def from_behind(value, axis, by):
    length = lax.axis_size(axis)
    return lax.ppermute(value, axis, [(i, (i + by) % length) for i in range(length)])


def swapped(value, axis, apart):
    mask = 2**apart
    pairs = [(source, source ^ mask) for source in range(lax.axis_size(axis))]
    return lax.ppermute(value, axis, pairs)


def shifted(value, axis, steps):
    count = lax.axis_size(axis)
    first, last = (max(0, -steps), min(count, count - steps))
    return lax.ppermute(value, axis, [(source, source + steps) for source in range(first, last)])


def noise_level(timesteps):
    phase_arg = (timesteps.astype(jnp.float32) / 1000.0 + 0.008) / 1.008
    return jnp.cos(phase_arg * (math.pi / 2.0)) ** 2


def norm_act(values, gain_rows):
    batch_size = values.shape[0]
    channels = values.shape[-1]
    grouped = values.reshape(batch_size, -1, GROUPS, channels // GROUPS)
    center = grouped - jnp.mean(grouped, axis=(1, 3), keepdims=True)
    spread = jnp.mean(center * center, axis=(1, 3), keepdims=True)
    normed = (center * lax.rsqrt(spread + 1e-05)).reshape(values.shape)
    return jax.nn.silu(normed * gain_rows[:, None, None, None, :])


def spatial_columns(activation):
    grid_height = activation.shape[2]
    grid_width = activation.shape[3]
    padded = jnp.pad(activation, ((0, 0), (0, 0), (1, 1), (1, 1), (0, 0)))
    pieces = [
        padded[:, :, row_shift : row_shift + grid_height, col_shift : col_shift + grid_width, :]
        for row_shift in range(3)
        for col_shift in range(3)
    ]
    return jnp.concatenate(pieces, axis=-1).reshape(-1, 9 * activation.shape[-1])


def spatial_spread(columns, full_shape):
    batch_size, frames, grid_height, grid_width, channels = full_shape
    columns = columns.reshape(batch_size, frames, grid_height, grid_width, 9, channels)
    summed = jnp.zeros((batch_size, frames, grid_height + 2, grid_width + 2, channels), jnp.float32)
    for kernel_tap in range(9):
        row_shift = kernel_tap // 3
        col_shift = kernel_tap % 3
        summed = summed + jnp.pad(
            columns[:, :, :, :, kernel_tap, :],
            ((0, 0), (0, 0), (row_shift, 2 - row_shift), (col_shift, 2 - col_shift), (0, 0)),
        )
    return summed[:, :, 1 : grid_height + 1, 1 : grid_width + 1, :]


def temporal_columns(activation):
    frames = activation.shape[1]
    padded = jnp.pad(activation, ((0, 0), (1, 1), (0, 0), (0, 0), (0, 0)))
    pieces = [padded[:, frame_shift : frame_shift + frames] for frame_shift in range(3)]
    return jnp.concatenate(pieces, axis=-1).reshape(-1, 3 * activation.shape[-1])


def temporal_spread(columns, full_shape):
    batch_size, frames, grid_height, grid_width, channels = full_shape
    columns = columns.reshape(batch_size, frames, grid_height, grid_width, 3, channels)
    summed = jnp.zeros((batch_size, frames + 2, grid_height, grid_width, channels), jnp.float32)
    for kernel_tap in range(3):
        summed = summed + jnp.pad(
            columns[:, :, :, :, kernel_tap, :],
            ((0, 0), (kernel_tap, 2 - kernel_tap), (0, 0), (0, 0), (0, 0)),
        )
    return summed[:, 1 : frames + 1]


def gate_shape(keep_rate):
    return keep_rate[:, None, None, None, None]


def encoder_forward(stream, weight, gain_rows, keep_rate):
    activation = norm_act(stream.astype(jnp.float32), gain_rows).astype(jnp.bfloat16)
    branch = jnp.dot(spatial_columns(activation), weight, preferred_element_type=jnp.float32)
    return (
        stream.astype(jnp.float32) + gate_shape(keep_rate) * branch.reshape(stream.shape)
    ).astype(jnp.bfloat16)


def encoder_backward(stream, upstream, weight, gain_rows, keep_rate):
    activation, pullback = jax.vjp(norm_act, stream.astype(jnp.float32), gain_rows)
    gated = (gate_shape(keep_rate) * upstream.astype(jnp.float32)).astype(jnp.bfloat16)
    back_cols = lax.dot_general(
        gated.reshape(-1, stream.shape[-1]),
        weight,
        (((1,), (1,)), ((), ())),
        preferred_element_type=jnp.float32,
    )
    norm_grad, gain_grad = pullback(spatial_spread(back_cols, stream.shape))
    stream_grad = (upstream.astype(jnp.float32) + norm_grad).astype(jnp.bfloat16)
    return (stream_grad, activation.astype(jnp.bfloat16), gated, gain_grad)


def decoder_forward(stream, skip_act, weight, gain_rows, keep_rate):
    merged = stream.astype(jnp.float32) + skip_act.astype(jnp.float32)
    activation = norm_act(merged, gain_rows).astype(jnp.bfloat16)
    branch = jnp.dot(temporal_columns(activation), weight, preferred_element_type=jnp.float32)
    return (
        stream.astype(jnp.float32) + gate_shape(keep_rate) * branch.reshape(stream.shape)
    ).astype(jnp.bfloat16)


def decoder_backward(stream, skip_act, upstream, weight, gain_rows, keep_rate):
    merged = stream.astype(jnp.float32) + skip_act.astype(jnp.float32)
    activation, pullback = jax.vjp(norm_act, merged, gain_rows)
    gated = (gate_shape(keep_rate) * upstream.astype(jnp.float32)).astype(jnp.bfloat16)
    back_cols = lax.dot_general(
        gated.reshape(-1, stream.shape[-1]),
        weight,
        (((1,), (1,)), ((), ())),
        preferred_element_type=jnp.float32,
    )
    merged_grad, gain_grad = pullback(temporal_spread(back_cols, stream.shape))
    stream_grad = (upstream.astype(jnp.float32) + merged_grad).astype(jnp.bfloat16)
    return (
        stream_grad,
        merged_grad.astype(jnp.bfloat16),
        activation.astype(jnp.bfloat16),
        gated,
        gain_grad,
    )


def weight_term(columns, gated):
    return lax.dot_general(
        columns, gated, (((0,), (0,)), ((), ())), preferred_element_type=jnp.float32
    )


def pick(stack, index):
    return lax.dynamic_slice_in_dim(stack, index, 1, 0)


def place(stack, piece, index, active):
    return jnp.where(active, lax.dynamic_update_slice_in_dim(stack, piece, index, 0), stack)


def body(
    clip_pool,
    sample_ids,
    timesteps,
    noise_draw,
    keep_lists,
    enc_weight,
    enc_gain,
    dec_weight,
    dec_gain,
):
    sections = lax.axis_size("section")
    own_level = lax.axis_index("section")
    micro_count = noise_draw.shape[0]
    channels = noise_draw.shape[-1]
    loop_len = sections + micro_count - 1
    last_level = sections - 1
    bit_count = sections.bit_length() - 1
    enc_kernel = enc_weight[0]
    dec_kernel = dec_weight[0]
    keep_rates = keep_lists.astype(jnp.float32)
    enc_keep = lax.dynamic_slice_in_dim(keep_rates, own_level, 1, 1)[:, 0]
    dec_keep = lax.dynamic_slice_in_dim(keep_rates, own_level + sections, 1, 1)[:, 0]
    clean = jnp.take(clip_pool, sample_ids, axis=0).astype(jnp.float32)
    level_noise = noise_level(timesteps)[:, None, None, None, None]
    inputs = (
        jnp.sqrt(level_noise) * clean + jnp.sqrt(1.0 - level_noise) * noise_draw.astype(jnp.float32)
    ).astype(jnp.bfloat16)
    blank = jnp.zeros((1,) + noise_draw.shape[1:], jnp.bfloat16)
    store_blank = jnp.zeros(noise_draw.shape, jnp.bfloat16)

    def slot_of(item_index):
        active = (item_index >= 0) & (item_index < micro_count)
        return (active, jnp.clip(item_index, 0, micro_count - 1))

    def encoder_step(step_index, loop_state):
        incoming, enc_inputs, enc_outputs, bottom = loop_state
        active, slot_index = slot_of(step_index - own_level)
        given = jnp.where(own_level == 0, pick(inputs, slot_index), incoming)
        keep_here = pick(enc_keep, slot_index)
        result = lax.cond(
            active,
            lambda operand: encoder_forward(operand, enc_kernel, enc_gain, keep_here),
            lambda operand: operand,
            given,
        )
        enc_inputs = place(enc_inputs, given, slot_index, active)
        enc_outputs = place(enc_outputs, result, slot_index, active)
        passed = from_behind(result, "section", 1)
        arrived, wrap_slot = slot_of(step_index - last_level)
        bottom = place(bottom, passed, wrap_slot, arrived & (own_level == 0))
        return (passed, enc_inputs, enc_outputs, bottom)

    leftover, enc_inputs, enc_outputs, bottom = lax.fori_loop(
        0, loop_len, encoder_step, (blank, store_blank, store_blank, store_blank)
    )
    skip_acts = enc_outputs
    for bit_index in range(bit_count):
        skip_acts = swapped(skip_acts, "section", bit_index)
    dec_first = 0
    dec_source = bottom

    def decoder_step(step_index, loop_state):
        incoming, dec_inputs, dec_outputs = loop_state
        active, slot_index = slot_of(step_index - own_level)
        given = jnp.where(own_level == dec_first, pick(dec_source, slot_index), incoming)
        skip_here = pick(skip_acts, slot_index)
        keep_here = pick(dec_keep, slot_index)
        result = lax.cond(
            active,
            lambda operand: decoder_forward(operand, skip_here, dec_kernel, dec_gain, keep_here),
            lambda operand: operand,
            given,
        )
        dec_inputs = place(dec_inputs, given, slot_index, active)
        dec_outputs = place(dec_outputs, result, slot_index, active)
        passed = shifted(result, "section", 1)
        return (passed, dec_inputs, dec_outputs)

    leftover, dec_inputs, dec_outputs = lax.fori_loop(
        0, loop_len, decoder_step, (blank, store_blank, store_blank)
    )
    positions = noise_draw.shape[1] * noise_draw.shape[2] * noise_draw.shape[3]
    scale = 1.0 / math.sqrt(micro_count * lax.axis_size("dp") * positions)
    loss_grads = (
        (dec_outputs.astype(jnp.float32) - noise_draw.astype(jnp.float32)) * scale
    ).astype(jnp.bfloat16)
    gain_blank = jnp.zeros(enc_gain.shape, jnp.float32)
    back_order = last_level - own_level

    def decoder_back_step(step_index, loop_state):
        incoming, skip_grads, bottom_grads, act_store, gated_store, gain_acc = loop_state
        active, slot_index = slot_of(step_index - back_order)
        given = jnp.where(own_level == last_level, pick(loss_grads, slot_index), incoming)
        keep_here = pick(dec_keep, slot_index)

        def decoder_run(operand):
            stream_grad, skip_grad, activation, gated, gain_grad = decoder_backward(
                pick(dec_inputs, slot_index),
                pick(skip_acts, slot_index),
                operand,
                dec_kernel,
                dec_gain,
                keep_here,
            )
            return (stream_grad, skip_grad, activation, gated, gain_acc + gain_grad)

        def decoder_rest(operand):
            return (operand, operand, operand, operand, gain_acc)

        stream_grad, skip_grad, activation, gated, gain_acc = lax.cond(
            active, decoder_run, decoder_rest, given
        )
        skip_grads = place(skip_grads, skip_grad, slot_index, active)
        act_store = place(act_store, activation, slot_index, active)
        gated_store = place(gated_store, gated, slot_index, active)
        passed = from_behind(stream_grad, "section", -1)
        arrived, wrap_slot = slot_of(step_index - last_level)
        bottom_grads = place(bottom_grads, passed, wrap_slot, arrived & (own_level == last_level))
        return (passed, skip_grads, bottom_grads, act_store, gated_store, gain_acc)

    leftover, skip_grads, bottom_grads, dec_acts, dec_gated, dec_gain_acc = lax.fori_loop(
        0,
        loop_len,
        decoder_back_step,
        (blank, store_blank, store_blank, store_blank, store_blank, gain_blank),
    )
    dec_weight_acc = weight_term(temporal_columns(dec_acts), dec_gated.reshape(-1, channels))
    skip_cots = skip_grads
    for bit_index in range(bit_count):
        skip_cots = swapped(skip_cots, "section", bit_index)

    def encoder_back_step(step_index, loop_state):
        incoming, act_store, gated_store, gain_acc = loop_state
        active, slot_index = slot_of(step_index - (last_level - own_level))
        given = jnp.where(own_level == last_level, pick(bottom_grads, slot_index), incoming)
        keep_here = pick(enc_keep, slot_index)

        def encoder_run(operand):
            summed_grad = (
                operand.astype(jnp.float32) + pick(skip_cots, slot_index).astype(jnp.float32)
            ).astype(jnp.bfloat16)
            stream_grad, activation, gated, gain_grad = encoder_backward(
                pick(enc_inputs, slot_index), summed_grad, enc_kernel, enc_gain, keep_here
            )
            return (stream_grad, activation, gated, gain_acc + gain_grad)

        def encoder_rest(operand):
            return (operand, operand, operand, gain_acc)

        stream_grad, activation, gated, gain_acc = lax.cond(
            active, encoder_run, encoder_rest, given
        )
        act_store = place(act_store, activation, slot_index, active)
        gated_store = place(gated_store, gated, slot_index, active)
        passed = shifted(stream_grad, "section", -1)
        return (passed, act_store, gated_store, gain_acc)

    leftover, enc_acts, enc_gated, enc_gain_acc = lax.fori_loop(
        0, loop_len, encoder_back_step, (blank, store_blank, store_blank, gain_blank)
    )
    enc_weight_acc = weight_term(spatial_columns(enc_acts), enc_gated.reshape(-1, channels))
    enc_weight_out, enc_gain_out, dec_weight_out, dec_gain_out = (
        lax.psum_scatter(
            enc_weight_acc.astype(jnp.bfloat16), "dp", scatter_dimension=0, tiled=True
        ).astype(jnp.float32),
        lax.psum_scatter(
            enc_gain_acc.astype(jnp.bfloat16), "dp", scatter_dimension=1, tiled=True
        ).astype(jnp.float32),
        lax.psum_scatter(
            dec_weight_acc.astype(jnp.bfloat16), "dp", scatter_dimension=0, tiled=True
        ).astype(jnp.float32),
        lax.psum_scatter(
            dec_gain_acc.astype(jnp.bfloat16), "dp", scatter_dimension=1, tiled=True
        ).astype(jnp.float32),
    )
    return (enc_weight_out[None], enc_gain_out, dec_weight_out[None], dec_gain_out)


def solution(mesh):
    placed = (
        P("dp", None, None, None, None),
        P("dp"),
        P("dp"),
        P("dp", None, None, None, None),
        P("dp", None),
        P("section", None, None),
        P("section", None),
        P("section", None, None),
        P("section", None),
    )
    return jax.shard_map(
        body,
        mesh=mesh,
        in_specs=placed,
        out_specs=(
            P("section", "dp", None),
            P("section", "dp"),
            P("section", "dp", None),
            P("section", "dp"),
        ),
        check_vma=False,
    )
```

profile of v0, /device:TPU:1, one launch (start us, length us, event | category | flops | bytes accessed | tf_op | source)
XLA Modules:
  0.0 1444.3 jit_solution(5328233168608197696)
XLA Ops:
  13.7 273.1 %while.85 = (s32[]{:T(128)}, bf16[1,3,4,2,640]{4,2,3,1,0:T(4,128)(2,1)S(1)}, bf16[8,3,4,2,640]{4,2,3,1,0:T(4,128)(2,1)S(1)}, bf16[8,3,4,2,640]{4,2,3,1,0:T(4,128...) while((s32[]{:T(128)}, ...), condition=%wide.region_7.8_spmd, body=%wide.region_0.7_spmd.sunk | while | flops 177438752 | bytes 8974227 | solution.py:211
  13.8 7.6 conditional.8
  28.0 7.6 conditional.8
  42.1 7.6 conditional.8
  56.2 7.6 conditional.8
  70.4 7.6 conditional.8
  84.5 7.6 conditional.8
  98.7 7.6 conditional.8
  112.8 7.6 conditional.8
  140.6 6.4 collective-permute-start
  190.4 11.1 collective-permute-done
  203.1 13.0 collective-permute-done
  217.8 12.3 collective-permute-done
  231.7 12.1 collective-permute-done
  245.5 13.0 collective-permute-done
  260.2 12.5 collective-permute-done
  274.3 12.5 collective-permute-done
  287.0 6.7 collective-permute-done.4
  298.8 8.3 collective-permute-done.6
  307.2 9.5 collective-permute-done.7
  317.6 206.8 %while.86 = (s32[]{:T(128)}, bf16[1,3,4,2,640]{4,2,3,1,0:T(4,128)(2,1)S(1)}, bf16[8,3,4,2,640]{4,2,3,1,0:T(4,128)(2,1)S(1)}, bf16[8,3,4,2,640]{4,3,2,1,0:T(2,128...) while((s32[]{:T(128)}, ...), condition=%wide.region_15.16_spmd, body=%wide.region_8.15_spmd.sunk | while | flops 59689000 | bytes 3463006 | solution.py:237
  397.1 8.4 collective-permute-start.1
  415.6 8.4 collective-permute-start.1
  513.3 9.6 collective-permute-start.1
  529.5 309.2 %while.87 = (s32[]{:T(128)}, bf16[1,3,4,2,640]{4,2,3,1,0:T(4,128)(2,1)S(1)}, bf16[8,3,4,2,640]{4,2,3,1,0:T(4,128)(2,1)}, bf16[8,3,4,2,640]{4,2,3,1,0:T(4,128)(2,...) while((s32[]{:T(128)}, ...), condition=%wide.region_28.29_spmd, body=%wide.region_16.28_spmd.sunk | while | flops 59858156 | bytes 4783309 | solution.py:279
  531.6 26.0 %collective-permute-start.2 = (bf16[1,3,4,2,640]{4,2,3,1,0:T(4,128)(2,1)S(1)}, bf16[1,3,4,2,640]{4,2,3,1,0:T(4,128)(2,1)S(1)}, u32[]{:S(2)}, u32[]{:S(2)}) collective-permute-start(bf16[1,3,4,2,640]{4,2,3,1,0:T(4,128)(2,1)S(1)} %get-tuple-element.1836), channel_id=1, source_target_pairs={{0,240},{16,0},{32,16},{48,32},{64,48},{80,64},{96,80},{112,96},{1... | collective-permute-start | bytes 92168 | tf_op jit(solution)/shard_map/while/body/eval_jaxpr/ppermute | solution.py:13
  563.9 8.3 collective-permute-start.2
  578.5 8.3 collective-permute-start.2
  593.1 8.3 collective-permute-start.2
  607.8 8.3 collective-permute-start.2
  622.4 8.3 collective-permute-start.2
  637.0 8.3 collective-permute-start.2
  651.6 8.3 collective-permute-start.2
  851.9 7.3 collective-permute-done.10
  868.4 373.1 %while.88 = (s32[]{:T(128)}, bf16[1,3,4,2,640]{4,2,3,1,0:T(4,128)(2,1)S(1)}, bf16[8,3,4,2,640]{4,2,3,1,0:T(4,128)(2,1)S(1)}, bf16[8,3,4,2,640]{4,2,3,1,0:T(4,128...) while((s32[]{:T(128)}, ...), condition=%wide.region_41.42_spmd, body=%wide.region_29.41_spmd.sunk | while | flops 178053344 | bytes 10936407 | solution.py:316
  954.4 6.5 collective-permute-done.3
  989.7 107.1 %collective-permute-done.3 = bf16[1,3,4,2,640]{4,2,3,1,0:T(4,128)(2,1)S(1)} collective-permute-done((bf16[1,3,4,2,640]{4,2,3,1,0:T(4,128)(2,1)S(1)}, bf16[1,3,4,2,640]{4,2,3,1,0:T(4,128)(2,1)S(1)}, u32[]{:S(2)}, u32[]{:S(2)}) %collective-permute-start.3) | collective-permute-done | bytes 30752 | tf_op jit(solution)/shard_map/while/body/eval_jaxpr/ppermute | solution.py:25
  1097.6 9.4 conditional.11
  1114.9 9.4 conditional.11
  1133.3 9.4 conditional.11
  1151.8 9.4 conditional.11
  1170.2 9.4 conditional.11
  1181.8 6.5 collective-permute-done.3
  1189.1 9.4 conditional.11
  1207.5 9.4 conditional.11
  1226.0 9.4 conditional.11
  1249.4 136.4 %all-reduce.20 = (bf16[1,640]{1,0:T(2,128)(2,1)S(1)}, bf16[1,640]{1,0:T(2,128)(2,1)S(1)}) all-reduce(bf16[1,640]{1,0:T(2,128)(2,1)S(1)} %convert_element_type.222, bf16[1,640]{1,0:T(2,128)(2,1)S(1)} %convert_element_type.225), channel_id=3, replica_groups=mesh['section'=16,'dp'=16] {'dp'}, use_global_device_ids=true, to_apply=%region_43.44.clone | all-reduce | flops 1280 | bytes 5120
  1388.0 47.4 %reduce-scatter.11.cloned.1.call-done = bf16[360,640]{1,0:T(8,128)(2,1)} async-done(((bf16[5760,640]{1,0:T(8,128)(2,1)}), bf16[360,640]{1,0:T(8,128)(2,1)}) %reduce-scatter.11.cloned.1.call-update) | async-done | bytes 460816
  (1603 shorter events, 968.6 us)
Async XLA Ops:
  7.2 1379.2 %reduce-scatter.13.cloned.1.call-start = ((), (), s32[]{:S(2)}) async-start(), calls=%async_computation.3 | async-start | bytes 2611200
  140.6 7.8 collective-permute-start
  168.9 7.8 collective-permute-start
  176.9 10.4 collective-permute-start
  187.5 14.0 collective-permute-start
  201.6 14.5 %collective-permute-start = (bf16[1,3,4,2,640]{4,2,3,1,0:T(4,128)(2,1)S(1)}, bf16[1,3,4,2,640]{4,2,3,1,0:T(4,128)(2,1)S(1)}, u32[]{:S(2)}, u32[]{:S(2)}) collective-permute-start(bf16[1,3,4,2,640]{4,2,3,1,0:T(4,128)(2,1)S(1)} %get-tuple-element.2084), channel_id=1, source_target_pairs={{0,16},{16,32},{32,48},{48,64},{64,80},{80,96},{96,112},{112,128},... | collective-permute-start | bytes 92168 | tf_op jit(solution)/shard_map/while/body/eval_jaxpr/ppermute | solution.py:13
  216.3 13.7 collective-permute-start
  230.3 13.6 collective-permute-start
  244.0 14.5 %collective-permute-start = (bf16[1,3,4,2,640]{4,2,3,1,0:T(4,128)(2,1)S(1)}, bf16[1,3,4,2,640]{4,2,3,1,0:T(4,128)(2,1)S(1)}, u32[]{:S(2)}, u32[]{:S(2)}) collective-permute-start(bf16[1,3,4,2,640]{4,2,3,1,0:T(4,128)(2,1)S(1)} %get-tuple-element.2084), channel_id=1, source_target_pairs={{0,16},{16,32},{32,48},{48,64},{64,80},{80,96},{96,112},{112,128},... | collective-permute-start | bytes 92168 | tf_op jit(solution)/shard_map/while/body/eval_jaxpr/ppermute | solution.py:13
  258.7 14.0 collective-permute-start
  272.8 14.0 collective-permute-start
  298.8 8.3 collective-permute-start.6
  307.1 9.6 collective-permute-start.7
  378.2 7.0 collective-permute-start.1
  388.9 7.4 collective-permute-start.1
  397.1 9.9 collective-permute-start.1
  407.8 7.0 collective-permute-start.1
  415.6 9.9 collective-permute-start.1
  426.3 7.0 collective-permute-start.1
  434.2 7.0 collective-permute-start.1
  504.9 7.6 collective-permute-start.1
  513.3 11.1 collective-permute-start.1
  531.6 28.8 %collective-permute-start.2 = (bf16[1,3,4,2,640]{4,2,3,1,0:T(4,128)(2,1)S(1)}, bf16[1,3,4,2,640]{4,2,3,1,0:T(4,128)(2,1)S(1)}, u32[]{:S(2)}, u32[]{:S(2)}) collective-permute-start(bf16[1,3,4,2,640]{4,2,3,1,0:T(4,128)(2,1)S(1)} %get-tuple-element.1836), channel_id=1, source_target_pairs={{0,240},{16,0},{32,16},{48,32},{64,48},{80,64},{96,80},{112,96},{1... | collective-permute-start | bytes 92168 | tf_op jit(solution)/shard_map/while/body/eval_jaxpr/ppermute | solution.py:13
  563.9 11.1 collective-permute-start.2
  578.5 11.1 collective-permute-start.2
  593.1 11.2 collective-permute-start.2
  607.8 11.1 collective-permute-start.2
  622.4 11.1 collective-permute-start.2
  637.0 11.1 collective-permute-start.2
  651.6 11.1 collective-permute-start.2
  838.7 7.1 collective-permute-start.8
  850.9 8.3 collective-permute-start.10
  859.2 9.1 collective-permute-start.11
  862.7 572.8 %reduce-scatter.11.cloned.1.call-start = ((), (), s32[]{:S(2)}) async-start(), calls=%async_computation.2 | async-start | bytes 7833600
  918.8 7.6 collective-permute-start.3
  944.2 7.4 collective-permute-start.3
  953.0 7.8 collective-permute-start.3
  962.3 7.2 collective-permute-start.3
  971.0 7.4 collective-permute-start.3
  979.8 7.1 collective-permute-start.3
  988.3 108.5 %collective-permute-start.3 = (bf16[1,3,4,2,640]{4,2,3,1,0:T(4,128)(2,1)S(1)}, bf16[1,3,4,2,640]{4,2,3,1,0:T(4,128)(2,1)S(1)}, u32[]{:S(2)}, u32[]{:S(2)}) collective-permute-start(bf16[1,3,4,2,640]{4,2,3,1,0:T(4,128)(2,1)S(1)} %get-tuple-element.1856), channel_id=1, source_target_pairs={{16,0},{32,16},{48,32},{64,48},{80,64},{96,80},{112,96},{128,112},... | collective-permute-start | bytes 92168 | tf_op jit(solution)/shard_map/while/body/eval_jaxpr/ppermute | solution.py:25
  1107.0 7.1 collective-permute-start.3
  1124.3 8.3 collective-permute-start.3
  1142.8 8.2 collective-permute-start.3
  1161.2 8.3 collective-permute-start.3
  1179.7 8.6 collective-permute-start.3
  1198.5 8.2 collective-permute-start.3
  1216.9 8.3 collective-permute-start.3
  (83 other events, 980.1 us)
Sparse Core Ops, SparseCore 0:
  862.8 148.0 reduce-scatter.12
  1247.6 187.8 reduce-scatter.10
where the time goes:
time: 1460 us; the launch traced here: 1440 us
  waiting for transfers between devices  485 us (33%)
  starting transfers between devices  314 us (22%)
  other arithmetic  233 us (16%)
  local copies, waits for them, and re-layouts  142 us (10%)
  blocking collectives  136 us (9%)
  matrix products  112 us (8%)
  between operations  14.9 us (1%)
    ppermute x46, waiting for transfers between devices, shifted(): lax.ppermute(value, axis, [(source, source + steps) for source in range(f...  233 us
    ppermute x46, starting transfers between devices, shifted(): lax.ppermute(value, axis, [(source, source + steps) for source in range(f...  161 us
    select_n x207, other arithmetic, place(): jnp.where(active, lax.dynamic_update_slice_in_dim(stack, piece, index, 0)...  157 us
    ppermute x46, waiting for transfers between devices, from_behind(): lax.ppermute(value, axis, [(i, (i + by) % length) for i in range(length)])  152 us
    ppermute x46, starting transfers between devices, from_behind(): lax.ppermute(value, axis, [(i, (i + by) % length) for i in range(length)])  151 us
    unnamed x1, blocking collectives  136 us
    ppermute x8, waiting for transfers between devices, swapped(): return lax.ppermute(value, axis, pairs)  53.1 us
    unnamed x4, waiting for transfers between devices  47.5 us
  transfers between devices with their start and end apart: 102, of which 59 were waited for; matrix products, arithmetic and copies ran while one was open for 17% of the time, Pallas kernels for 0%

commit v1 on v0

v1 whole, which is shorter than its diff:
```python
import math

import jax
import jax.numpy as jnp
import numpy as np
from jax import lax
from jax.experimental import pallas as pl
from jax.experimental.pallas import tpu as pltpu
from jax.sharding import PartitionSpec as P

GROUPS = 32
F32, BF16 = jnp.float32, jnp.bfloat16
MESH = pl.DeviceIdType.MESH
PACE = 2


def noise_level(timesteps):
    phase_arg = (timesteps.astype(F32) / 1000.0 + 0.008) / 1.008
    return jnp.cos(phase_arg * (math.pi / 2.0)) ** 2


def over_rows(values):
    part = values[0] + values[1] + values[2]
    return jnp.broadcast_to(jnp.sum(part, axis=0, keepdims=True), part.shape)


def split_terms(values):
    high = values.astype(BF16).astype(F32)
    rest = values - high
    middle = rest.astype(BF16).astype(F32)
    return [high, middle, rest - middle]


def group_means(rows, mix_ref, count):
    terms = [term for row in rows for term in split_terms(row)]
    stacked = jnp.concatenate(terms, axis=0).astype(BF16)
    sums = jnp.dot(stacked, mix_ref[...], preferred_element_type=F32)
    return [
        (sums[24 * i : 24 * i + 8] + sums[24 * i + 8 : 24 * i + 16] + sums[24 * i + 16 : 24 * i + 24])
        * (1.0 / count)
        for i in range(len(rows))
    ]


def cube(values):
    return values.reshape(3, 8, values.shape[-1])


def padded_rows(values):
    full = jnp.concatenate([values, jnp.zeros((1,) + values.shape[1:], F32)], axis=0)
    return full.reshape(32, values.shape[-1]).astype(BF16)


def spatial_taps(values, sign):
    place = lax.broadcasted_iota(jnp.int32, values.shape, 1)
    high, wide = place // 2, place % 2
    taps = []
    for tap in range(9):
        down, across = sign * (tap // 3 - 1), sign * (tap % 3 - 1)
        shift = 2 * down + across
        moved = pltpu.roll(values, (-shift) % 8, 1) if shift % 8 else values
        if down or across:
            inside = (
                (high + down >= 0) & (high + down < 4) & (wide + across >= 0) & (wide + across < 2)
            )
            moved = jnp.where(inside, moved, 0.0)
        taps.append(padded_rows(moved))
    return taps


def temporal_taps(values, sign):
    zero = jnp.zeros_like(values[:1])
    before = jnp.concatenate([zero, values[:2]], axis=0)
    after = jnp.concatenate([values[1:], zero], axis=0)
    taps = [before, values, after] if sign > 0 else [after, values, before]
    return [padded_rows(tap) for tap in taps]


def norm_forward(values, gain, mix_ref, count):
    mean = group_means([over_rows(values)], mix_ref, count)[0]
    center = values - mean[None]
    spread = group_means([over_rows(center * center)], mix_ref, count)[0]
    scale = lax.rsqrt(spread + 1e-05)
    normed = center * scale[None]
    z = normed * gain[None]
    gate = 1.0 / (1.0 + jnp.exp(-z))
    return normed, scale, z, gate


def norm_backward(cot, normed, scale, slope, gain, mix_ref, count):
    dz = cot * slope
    gain_part = dz * normed
    gain_part = gain_part[0] + gain_part[1] + gain_part[2]
    dn = dz * gain[None]
    mean_dn, mean_dnn = group_means([over_rows(dn), over_rows(dn * normed)], mix_ref, count)
    return scale[None] * (dn - mean_dn[None] - normed * mean_dnn[None]), gain_part


def transposed_product(taps, weight_ref, channels):
    total = None
    for index, tap in enumerate(taps):
        part = lax.dot_general(
            tap,
            weight_ref[pl.ds(index * channels, channels), :],
            (((1,), (1,)), ((), ())),
            preferred_element_type=F32,
        )
        total = part if total is None else total + part
    return total


def pipeline_kernel(
    sections,
    micros,
    loss_scale,
    keep_ref,
    first_ref,
    noise_ref,
    enc_gain_ref,
    dec_gain_ref,
    mix_ref,
    enc_hbm,
    dec_hbm,
    dwe_ref,
    dwd_ref,
    dge_ref,
    dgd_ref,
    enc_w,
    dec_w,
    fwd_in,
    bwd_in,
    skip_in,
    scot_in,
    enc_out,
    dec_out,
    g_out,
    s_out,
    q_out,
    enc_normed,
    dec_normed,
    enc_slope,
    dec_slope,
    enc_scale,
    dec_scale,
    enc_act,
    dec_act,
    enc_cot,
    dec_cot,
    turned,
    local_sem,
    fwd_sem,
    bwd_sem,
    skip_sem,
    scot_sem,
    send_sem,
):
    channels = noise_ref.shape[-1]
    count = 24 * (channels // GROUPS)
    own = lax.axis_index("section")
    last = sections - 1
    after = lax.rem(own + 1, sections)
    before = lax.rem(own + last, sections)
    mirror = last - own
    wrap_up = (own + 1) // sections
    wrap_down = (last - own) // last

    load_enc = pltpu.make_async_copy(enc_hbm, enc_w, local_sem.at[0])
    load_dec = pltpu.make_async_copy(dec_hbm, dec_w, local_sem.at[1])
    load_enc.start()
    load_dec.start()

    barrier = pltpu.get_barrier_semaphore()
    for other in (after, before, mirror):
        pl.semaphore_signal(barrier, inc=1, device_id={"section": other}, device_id_type=MESH)
    pl.semaphore_wait(barrier, 3)

    @pl.when(own == 0)
    def _():
        for j in range(micros):
            fwd_in[j] = first_ref[j]

    dge_ref[...] = jnp.zeros_like(dge_ref)
    dgd_ref[...] = jnp.zeros_like(dgd_ref)
    load_enc.wait()
    load_dec.wait()

    def send(source, j, target, slot, arrive, kind, other):
        return pltpu.make_async_remote_copy(
            src_ref=source.at[j],
            dst_ref=target.at[slot],
            send_sem=send_sem.at[kind, j],
            recv_sem=arrive.at[slot],
            device_id={"section": other},
            device_id_type=MESH,
        )

    def arrived(buffer, slot, sem):
        pltpu.make_async_copy(buffer.at[slot], buffer.at[slot], sem.at[slot]).wait()

    def turn(source):
        turned[...] = source[...].astype(F32).T.astype(BF16)

    def step(t, carry):
        def window(start):
            j = t - start
            return j, (j >= 0) & (j < micros)

        j_ef, enc_fwd = window(own * PACE)

        @pl.when(enc_fwd)
        def _():
            j = j_ef

            @pl.when(own > 0)
            def _():
                arrived(fwd_in, j, fwd_sem)

            values = cube(fwd_in[j].astype(F32))
            keep = keep_ref[j, own].astype(F32)
            gain = enc_gain_ref[...]
            normed, scale, z, gate = norm_forward(values, gain, mix_ref, count)
            act = z * gate
            columns = jnp.concatenate(spatial_taps(act, 1), axis=1)
            branch = jnp.dot(columns, enc_w[...], preferred_element_type=F32)
            result = values + keep * cube(branch[:24])
            enc_out[j] = result.reshape(24, channels).astype(BF16)
            send(enc_out, j, fwd_in, j + micros * wrap_up, fwd_sem, 0, after).start()
            send(enc_out, j, skip_in, j, skip_sem, 1, mirror).start()
            enc_normed[j] = normed
            enc_scale[j] = scale
            enc_slope[j] = gate * (1.0 + z * (1.0 - gate))
            enc_act[pl.ds(pl.multiple_of(j * 32, 32), 32), :] = padded_rows(act)

        j_df, dec_fwd = window((sections + own) * PACE)

        @pl.when(dec_fwd)
        def _():
            j = j_df
            arrived(fwd_in, micros + j, fwd_sem)
            arrived(skip_in, j, skip_sem)
            stream = cube(fwd_in[micros + j].astype(F32))
            values = stream + cube(skip_in[j].astype(F32))
            keep = keep_ref[j, sections + own].astype(F32)
            gain = dec_gain_ref[...]
            normed, scale, z, gate = norm_forward(values, gain, mix_ref, count)
            act = z * gate
            columns = jnp.concatenate(temporal_taps(act, 1), axis=1)
            branch = jnp.dot(columns, dec_w[...], preferred_element_type=F32)
            result = (stream + keep * cube(branch[:24])).reshape(24, channels).astype(BF16)
            dec_out[j] = result

            @pl.when(own < last)
            def _():
                send(dec_out, j, fwd_in, micros + j, fwd_sem, 2, after).start()

            @pl.when(own == last)
            def _():
                gap = result.astype(F32) - noise_ref[j].astype(F32)
                bwd_in[j] = (gap * loss_scale).astype(BF16)

            dec_normed[j] = normed
            dec_scale[j] = scale
            dec_slope[j] = gate * (1.0 + z * (1.0 - gate))
            dec_act[pl.ds(pl.multiple_of(j * 32, 32), 32), :] = padded_rows(act)

        j_db, dec_bwd = window((3 * sections - 2 - own) * PACE)

        @pl.when(dec_bwd)
        def _():
            j = j_db

            @pl.when(own < last)
            def _():
                arrived(bwd_in, j, bwd_sem)

            upstream = cube(bwd_in[j].astype(F32))
            keep = keep_ref[j, sections + own].astype(F32)
            taps = temporal_taps(keep * upstream, -1)
            cot = cube(transposed_product(taps, dec_w, channels)[:24])
            grad, gain_part = norm_backward(
                cot, dec_normed[j], dec_scale[j], dec_slope[j], dec_gain_ref[...], mix_ref, count
            )
            g_out[j] = (upstream + grad).reshape(24, channels).astype(BF16)
            send(g_out, j, bwd_in, j + micros * wrap_down, bwd_sem, 3, before).start()
            s_out[j] = grad.reshape(24, channels).astype(BF16)
            send(s_out, j, scot_in, j, scot_sem, 4, mirror).start()
            dgd_ref[...] += gain_part
            dec_cot[pl.ds(pl.multiple_of(j * 32, 32), 32), :] = jnp.concatenate(taps, axis=1)

        @pl.when(t == (3 * sections - 2 - own) * PACE + micros)
        def _():
            turn(dec_act)
            for tap in range(3):
                dwd_ref[tap * channels : (tap + 1) * channels, :] = jnp.dot(
                    turned[...],
                    dec_cot[:, tap * channels : (tap + 1) * channels],
                    preferred_element_type=F32,
                ).astype(BF16)
            turn(enc_act)

        j_eb, enc_bwd = window((4 * sections - 2 - own) * PACE)

        @pl.when(enc_bwd)
        def _():
            j = j_eb
            arrived(scot_in, j, scot_sem)
            arrived(bwd_in, micros + j, bwd_sem)
            upstream = fwd_sum(bwd_in[micros + j], scot_in[j])
            keep = keep_ref[j, own].astype(F32)
            taps = spatial_taps(keep * upstream, -1)
            cot = cube(transposed_product(taps, enc_w, channels)[:24])
            grad, gain_part = norm_backward(
                cot, enc_normed[j], enc_scale[j], enc_slope[j], enc_gain_ref[...], mix_ref, count
            )

            @pl.when(own > 0)
            def _():
                q_out[j] = (upstream + grad).reshape(24, channels).astype(BF16)
                send(q_out, j, bwd_in, micros + j, bwd_sem, 5, before).start()

            dge_ref[...] += gain_part
            enc_cot[pl.ds(pl.multiple_of(j * 32, 32), 32), :] = jnp.concatenate(taps, axis=1)

        return carry

    def fwd_sum(stream, skip):
        return cube((stream.astype(F32) + skip.astype(F32)).astype(BF16).astype(F32))

    lax.fori_loop(0, (4 * sections - 2) * PACE + micros, step, 0)
    for tap in range(9):
        dwe_ref[tap * channels : (tap + 1) * channels, :] = jnp.dot(
            turned[...],
            enc_cot[:, tap * channels : (tap + 1) * channels],
            preferred_element_type=F32,
        ).astype(BF16)

    def drain(j, carry):
        for kind, source in ((0, enc_out), (1, enc_out), (3, g_out), (4, s_out)):
            pltpu.make_async_copy(source.at[j], source.at[j], send_sem.at[kind, j]).wait()

        @pl.when(own < last)
        def _():
            pltpu.make_async_copy(dec_out.at[j], dec_out.at[j], send_sem.at[2, j]).wait()

        @pl.when(own > 0)
        def _():
            pltpu.make_async_copy(q_out.at[j], q_out.at[j], send_sem.at[5, j]).wait()

        return carry

    lax.fori_loop(0, micros, drain, 0)


def body(
    clip_pool,
    sample_ids,
    timesteps,
    noise_draw,
    keep_lists,
    enc_weight,
    enc_gain,
    dec_weight,
    dec_gain,
):
    sections = lax.axis_size("section")
    micros = noise_draw.shape[0]
    channels = noise_draw.shape[-1]
    positions = noise_draw.shape[1] * noise_draw.shape[2] * noise_draw.shape[3]
    scale = 1.0 / math.sqrt(micros * lax.axis_size("dp") * positions)
    flat = (micros, positions, channels)
    noise = noise_draw.reshape(flat)
    clips = clip_pool.reshape((-1,) + flat[1:])
    clean = jnp.zeros(flat, F32)
    for clip in range(clips.shape[0]):
        clean = jnp.where((sample_ids == clip)[:, None, None], clips[clip][None].astype(F32), clean)
    level = noise_level(timesteps)[:, None, None]
    first = (jnp.sqrt(level) * clean + jnp.sqrt(1.0 - level) * noise.astype(F32)).astype(BF16)
    member = np.arange(channels) // (channels // GROUPS)
    mix = jnp.asarray((member[:, None] == member[None, :]).astype(np.float32), BF16)
    vmem = pl.BlockSpec(memory_space=pltpu.VMEM)
    hbm = pl.BlockSpec(memory_space=pl.ANY)
    slots = lambda n: pltpu.VMEM((n, positions, channels), BF16)
    kept = lambda: pltpu.VMEM((micros, 3, 8, channels), F32)
    rows = 32 * micros
    dwe, dwd, dge, dgd = pl.pallas_call(
        lambda *refs: pipeline_kernel(sections, micros, scale, *refs),
        out_shape=(
            jax.ShapeDtypeStruct((9 * channels, channels), BF16),
            jax.ShapeDtypeStruct((3 * channels, channels), BF16),
            jax.ShapeDtypeStruct((8, channels), F32),
            jax.ShapeDtypeStruct((8, channels), F32),
        ),
        in_specs=[pl.BlockSpec(memory_space=pltpu.SMEM), vmem, vmem, vmem, vmem, vmem, hbm, hbm],
        out_specs=(vmem, vmem, vmem, vmem),
        scratch_shapes=[
            pltpu.VMEM((9 * channels, channels), BF16),
            pltpu.VMEM((3 * channels, channels), BF16),
            slots(2 * micros),
            slots(2 * micros),
            slots(micros),
            slots(micros),
            slots(micros),
            slots(micros),
            slots(micros),
            slots(micros),
            slots(micros),
            kept(),
            kept(),
            kept(),
            kept(),
            pltpu.VMEM((micros, 8, channels), F32),
            pltpu.VMEM((micros, 8, channels), F32),
            pltpu.VMEM((rows, channels), BF16),
            pltpu.VMEM((rows, channels), BF16),
            pltpu.VMEM((rows, 9 * channels), BF16),
            pltpu.VMEM((rows, 3 * channels), BF16),
            pltpu.VMEM((channels, rows), BF16),
            pltpu.SemaphoreType.DMA((2,)),
            pltpu.SemaphoreType.DMA((2 * micros,)),
            pltpu.SemaphoreType.DMA((2 * micros,)),
            pltpu.SemaphoreType.DMA((micros,)),
            pltpu.SemaphoreType.DMA((micros,)),
            pltpu.SemaphoreType.DMA((6, micros)),
        ],
        compiler_params=pltpu.CompilerParams(
            collective_id=0, has_side_effects=True, vmem_limit_bytes=56 << 20
        ),
        name="pipeline",
    )(keep_lists, first, noise, enc_gain, dec_gain, mix, enc_weight[0], dec_weight[0])
    gains = jnp.stack([jnp.sum(dge, axis=0), jnp.sum(dgd, axis=0)]).astype(BF16)
    scatter = lambda value, dim: lax.psum_scatter(
        value, "dp", scatter_dimension=dim, tiled=True
    ).astype(F32)
    dwe, dwd, gains = scatter(dwe, 0), scatter(dwd, 0), scatter(gains, 1)
    return (dwe[None], gains[:1], dwd[None], gains[1:])


def solution(mesh):
    placed = (
        P("dp", None, None, None, None),
        P("dp"),
        P("dp"),
        P("dp", None, None, None, None),
        P("dp", None),
        P("section", None, None),
        P("section", None),
        P("section", None, None),
        P("section", None),
    )
    return jax.shard_map(
        body,
        mesh=mesh,
        in_specs=placed,
        out_specs=(
            P("section", "dp", None),
            P("section", "dp"),
            P("section", "dp", None),
            P("section", "dp"),
        ),
        check_vma=False,
    )
```

time: 1460 us -> 559 us (0.38)
  waiting for transfers between devices: 485 us -> 122 us
  Pallas kernels: 0 us -> 332 us
  starting transfers between devices: 314 us -> 0.08 us
  other arithmetic: 233 us -> 7.1 us
  local copies, waits for them, and re-layouts: 142 us -> 2.36 us
  matrix products: 112 us -> 0 us
  blocking collectives: 136 us -> 80.1 us
    ppermute x100 -> x0, waiting for transfers between devices: 438 us -> none  [the longest x46 233 us: shifted(): lax.ppermute(value, axis, [(source, source + steps) for source in range(f...]
    pallas_call x0 -> x1, Pallas kernels: none -> 332 us  [body(): pl.pallas_call(lambda *refs: pipeline_kernel(sections, micros, scale, *re...]
    ppermute x100 -> x0, starting transfers between devices: 313 us -> none  [the longest x46 161 us: shifted(): lax.ppermute(value, axis, [(source, source + steps) for source in range(f...]
    select_n x254 -> x0, other arithmetic: 176 us -> none  [the longest x207 157 us: place(): jnp.where(active, lax.dynamic_update_slice_in_dim(stack, piece, index, 0)...]
    dot_general x34 -> x0, matrix products: 112 us -> none  [the longest x8 41.9 us: encoder_backward(): lax.dot_general(gated.reshape(-1, stream.shape[-1]), weight, (((1,), (1,)...]
    unnamed x4, waiting for transfers between devices: 47.5 us -> 122 us
    unnamed x1, blocking collectives: 136 us -> 80.1 us
    dynamic_slice x79 -> x0, local copies, waits for them, and re-layouts: 38.7 us -> none  [the longest x78 38.5 us: pick(): return lax.dynamic_slice_in_dim(stack, index, 1, 0)]
  transfers between devices with their start and end apart: 102 -> 2, of which waited for: 59 -> 2; matrix products, arithmetic and copies ran while one was open for 17% -> 1% of each run, Pallas kernels for 0% -> 0%
where the time goes in v1:
time: 559 us; the launch traced here: 558 us
  Pallas kernels  332 us (59%)
  waiting for transfers between devices  122 us (22%)
  blocking collectives  80.1 us (14%)
  between operations  14.8 us (3%)
  other arithmetic  7.1 us (1%)
    pallas_call x1, Pallas kernels, body(): pl.pallas_call(lambda *refs: pipeline_kernel(sections, micros, scale, *re...  332 us
    unnamed x4, waiting for transfers between devices  122 us
    unnamed x1, blocking collectives  80.1 us
  transfers between devices with their start and end apart: 2, of which 2 were waited for; matrix products, arithmetic and copies ran while one was open for 1% of the time, Pallas kernels for 0%

profile of v1, /device:TPU:1, one launch (start us, length us, event | category | flops | bytes accessed | tf_op | source)
XLA Modules:
  0.0 557.8 jit_solution(2530356615302280023)
XLA Ops:
  7.2 0.0 reduce-scatter.12.cloned.1.call-start
  7.2 0.9 slice_convert_fusion.3
  8.3 0.7 broadcast_compare_fusion.3
  9.0 1.0 reshape.61.refs_2_
  10.0 0.0 copy-start
  10.0 0.7 fusion
  10.8 1.0 add_convert_fusion.refs_1_
  11.8 0.0 copy-done
  11.8 331.6 %pipeline.1 = (bf16[5760,640]{1,0:T(8,128)(2,1)}, bf16[1920,640]{1,0:T(8,128)(2,1)}, f32[8,640]{1,0:T(8,128)}, f32[8,640]{1,0:T(8,128)}) custom-call(s32[8,32]{1,0:T(8,128)} %refs_0_.1, bf16[8,24,640]{2,1,0:T(8,128)(2,1)} %add_convert_fusion.refs_1_, bf16[8,24,640]{2,1,0:T(8,128)(2,1)} %copy-done, f32[1,640]{1,0:T(1,128)} %refs_3_.1, f32[1,640]{1,0:T(1,128)} %refs_4_.1, ...), custom_call_target="tpu_custom_call" | custom-call | tf_op jit(solution)/shard_map/pipeline/pallas_call | solution.py:385
  343.4 0.0 copy-start.2
  343.4 0.0 copy-start.1
  343.4 0.0 copy-start.3
  343.4 0.0 reduce-scatter.12.cloned.1.call-update
  343.4 0.0 reduce-scatter.10.cloned.1.call-start
  343.5 0.7 reduce-scatter.10.cloned.1.call-update
  344.2 0.0 copy-done.2
  344.2 0.0 copy-done.1
  344.3 0.0 copy-done.3
  344.3 0.6 dynamic-slice
  345.6 80.1 %all-reduce.1 = bf16[2,640]{1,0:T(2,128)(2,1)S(1)} all-reduce(bf16[2,640]{1,0:T(2,128)(2,1)S(1)} %pad_maximum_fusion), channel_id=3, replica_groups=mesh['section'=16,'dp'=16] {'dp'}, use_global_device_ids=true, to_apply=%region_3.4.clone | all-reduce | flops 1280 | bytes 5120
  425.7 0.1 dynamic-slice_convert_fusion
  425.8 0.5 fusion.1
  426.3 30.1 %reduce-scatter.12.cloned.1.call-done = bf16[120,640]{1,0:T(8,128)(2,1)} async-done(((bf16[1920,640]{1,0:T(8,128)(2,1)}), bf16[120,640]{1,0:T(8,128)(2,1)}) %reduce-scatter.12.cloned.1.call-update) | async-done | bytes 153616
  456.3 1.6 bitcast_convert_fusion.1
  458.0 91.0 %reduce-scatter.10.cloned.1.call-done = bf16[360,640]{1,0:T(8,128)(2,1)} async-done(((bf16[5760,640]{1,0:T(8,128)(2,1)}), bf16[360,640]{1,0:T(8,128)(2,1)}) %reduce-scatter.10.cloned.1.call-update) | async-done | bytes 460816
  548.9 2.0 bitcast_convert_fusion
  (9 shorter events, 0.2 us)
Async XLA Ops:
  7.2 449.2 %reduce-scatter.12.cloned.1.call-start = ((), (), s32[]{:S(2)}) async-start(), calls=%async_computation.3 | async-start | bytes 2611200
  10.0 1.8 copy-start
  343.4 0.8 copy-start.2
  343.4 0.9 copy-start.1
  343.4 0.9 copy-start.3
  343.4 205.5 %reduce-scatter.10.cloned.1.call-start = ((), (), s32[]{:S(2)}) async-start(), calls=%async_computation.2 | async-start | bytes 7833600
Sparse Core Ops, SparseCore 0:
  343.6 112.7 reduce-scatter.11
  458.9 89.9 reduce-scatter.9

commit v2 on v1

--- a/solution.py
+++ b/solution.py
@@ -96,17 +96,88 @@
     return scale[None] * (dn - mean_dn[None] - normed * mean_dnn[None]), gain_part
 
 
-def transposed_product(taps, weight_ref, channels):
-    total = None
-    for index, tap in enumerate(taps):
-        part = lax.dot_general(
-            tap,
-            weight_ref[pl.ds(index * channels, channels), :],
-            (((1,), (1,)), ((), ())),
+def scatter_start(p, c, sibling, dw, from_sibling, pair, from_chips, sems):
+    chips = dw.shape[0]
+    send_pair, arrive_pair, send_chip, arrive_chip = sems
+
+    def to_sibling(o, carry):
+        m = lax.rem(p + o, chips)
+        pltpu.make_async_remote_copy(
+            src_ref=dw.at[m, 1 - c],
+            dst_ref=from_sibling.at[m],
+            send_sem=send_pair.at[m],
+            recv_sem=arrive_pair.at[m],
+            device_id={"dp": sibling},
+            device_id_type=MESH,
+        ).start()
+        return carry
+
+    def to_chip(o, carry):
+        m = lax.rem(p + o, chips)
+        pltpu.make_async_copy(from_sibling.at[m], from_sibling.at[m], arrive_pair.at[m]).wait()
+
+        def add(block, inner):
+            pair[m, block] = (
+                dw[m, c, block].astype(F32) + from_sibling[m, block].astype(F32)
+            ).astype(BF16)
+            return inner
+
+        lax.fori_loop(0, dw.shape[2], add, 0)
+        pltpu.make_async_remote_copy(
+            src_ref=pair.at[m],
+            dst_ref=from_chips.at[o - 1],
+            send_sem=send_chip.at[o - 1],
+            recv_sem=arrive_chip.at[o - 1],
+            device_id={"dp": 2 * m + c},
+            device_id_type=MESH,
+        ).start()
+        return carry
+
+    lax.fori_loop(1, chips + 1, to_sibling, 0)
+    lax.fori_loop(1, chips, to_chip, 0)
+    pltpu.make_async_copy(from_sibling.at[p], from_sibling.at[p], arrive_pair.at[p]).wait()
+
+
+def scatter_end(p, c, dw, from_sibling, pair, from_chips, sems, out_ref):
+    chips = dw.shape[0]
+    send_pair, arrive_pair, send_chip, arrive_chip = sems
+
+    def arrive(o, carry):
+        pltpu.make_async_copy(from_chips.at[o], from_chips.at[o], arrive_chip.at[o]).wait()
+        return carry
+
+    def add(block, carry):
+        total = dw[p, c, block].astype(F32) + from_sibling[p, block].astype(F32)
+        for o in range(chips - 1):
+            total = total + from_chips[o, block].astype(F32)
+        out_ref[block] = total
+        return carry
+
+    def sent(o, carry):
+        pltpu.make_async_copy(pair.at[o], pair.at[o], send_chip.at[o]).wait()
+        return carry
+
+    def sent_pair(m, carry):
+        pltpu.make_async_copy(from_sibling.at[m], from_sibling.at[m], send_pair.at[m]).wait()
+        return carry
+
+    lax.fori_loop(0, chips - 1, arrive, 0)
+    lax.fori_loop(0, dw.shape[2], add, 0)
+    lax.fori_loop(0, chips - 1, sent, 0)
+    lax.fori_loop(0, chips, sent_pair, 0)
+
+
+def weight_terms(turned, cot, dw, channels):
+    blocks = dw.shape[2]
+    for tap in range(cot.shape[1] // channels):
+        part = jnp.dot(
+            turned[...],
+            cot[:, tap * channels : (tap + 1) * channels],
             preferred_element_type=F32,
-        )
-        total = part if total is None else total + part
-    return total
+        ).reshape(channels // 40, 40, channels)
+        for i in range(channels // 40):
+            at = tap * (channels // 40) + i
+            dw[at // (2 * blocks), (at // blocks) % 2, at % blocks] = part[i].astype(BF16)
 
 
 def pipeline_kernel(
@@ -121,12 +192,12 @@
     mix_ref,
     enc_hbm,
     dec_hbm,
-    dwe_ref,
-    dwd_ref,
-    dge_ref,
-    dgd_ref,
+    dwe_out,
+    dwd_out,
+    gain_out,
     enc_w,
     dec_w,
+    dec_wt,
     fwd_in,
     bwd_in,
     skip_in,
@@ -147,12 +218,32 @@
     enc_cot,
     dec_cot,
     turned,
+    dge_ref,
+    dgd_ref,
+    gain_own,
+    gain_pair,
+    gain_sibling,
+    gain_chips,
+    enc_dw,
+    enc_sibling,
+    enc_pair,
+    enc_chips,
+    dec_dw,
+    dec_sibling,
+    dec_pair,
+    dec_chips,
     local_sem,
     fwd_sem,
     bwd_sem,
     skip_sem,
     scot_sem,
     send_sem,
+    enc_pair_sem,
+    enc_chip_sem,
+    dec_pair_sem,
+    dec_chip_sem,
+    gain_pair_sem,
+    gain_chip_sem,
 ):
     channels = noise_ref.shape[-1]
     count = 24 * (channels // GROUPS)
@@ -169,10 +260,25 @@
     load_enc.start()
     load_dec.start()
 
+    dp = lax.axis_index("dp")
+    p, c = dp // 2, lax.rem(dp, 2)
+    sibling = dp + 1 - 2 * c
+    chips = enc_dw.shape[0]
+    enc_sems = [enc_pair_sem.at[0], enc_pair_sem.at[1], enc_chip_sem.at[0], enc_chip_sem.at[1]]
+    dec_sems = [dec_pair_sem.at[0], dec_pair_sem.at[1], dec_chip_sem.at[0], dec_chip_sem.at[1]]
+
     barrier = pltpu.get_barrier_semaphore()
     for other in (after, before, mirror):
         pl.semaphore_signal(barrier, inc=1, device_id={"section": other}, device_id_type=MESH)
-    pl.semaphore_wait(barrier, 3)
+    pl.semaphore_signal(barrier, inc=1, device_id={"dp": sibling}, device_id_type=MESH)
+    for o in range(1, chips):
+        pl.semaphore_signal(
+            barrier,
+            inc=1,
+            device_id={"dp": 2 * lax.rem(p + o, chips) + c},
+            device_id_type=MESH,
+        )
+    pl.semaphore_wait(barrier, 3 + chips)
 
     @pl.when(own == 0)
     def _():
@@ -231,6 +337,21 @@
             enc_slope[j] = gate * (1.0 + z * (1.0 - gate))
             enc_act[pl.ds(pl.multiple_of(j * 32, 32), 32), :] = padded_rows(act)
 
+        @pl.when(t == own * PACE + micros)
+        def _():
+            def tap_enc(tap, inner):
+                rows = pl.ds(pl.multiple_of(tap * channels, channels), channels)
+                enc_w[rows, :] = enc_w[rows, :].astype(F32).T.astype(BF16)
+                return inner
+
+            def tap_dec(tap, inner):
+                rows = pl.ds(pl.multiple_of(tap * channels, channels), channels)
+                dec_wt[rows, :] = dec_w[rows, :].astype(F32).T.astype(BF16)
+                return inner
+
+            lax.fori_loop(0, 9, tap_enc, 0)
+            lax.fori_loop(0, 3, tap_dec, 0)
+
         j_df, dec_fwd = window((sections + own) * PACE)
 
         @pl.when(dec_fwd)
@@ -276,7 +397,8 @@
             upstream = cube(bwd_in[j].astype(F32))
             keep = keep_ref[j, sections + own].astype(F32)
             taps = temporal_taps(keep * upstream, -1)
-            cot = cube(transposed_product(taps, dec_w, channels)[:24])
+            columns = jnp.concatenate(taps, axis=1)
+            cot = cube(jnp.dot(columns, dec_wt[...], preferred_element_type=F32)[:24])
             grad, gain_part = norm_backward(
                 cot, dec_normed[j], dec_scale[j], dec_slope[j], dec_gain_ref[...], mix_ref, count
             )
@@ -285,18 +407,14 @@
             s_out[j] = grad.reshape(24, channels).astype(BF16)
             send(s_out, j, scot_in, j, scot_sem, 4, mirror).start()
             dgd_ref[...] += gain_part
-            dec_cot[pl.ds(pl.multiple_of(j * 32, 32), 32), :] = jnp.concatenate(taps, axis=1)
+            dec_cot[pl.ds(pl.multiple_of(j * 32, 32), 32), :] = columns
 
         @pl.when(t == (3 * sections - 2 - own) * PACE + micros)
         def _():
             turn(dec_act)
-            for tap in range(3):
-                dwd_ref[tap * channels : (tap + 1) * channels, :] = jnp.dot(
-                    turned[...],
-                    dec_cot[:, tap * channels : (tap + 1) * channels],
-                    preferred_element_type=F32,
-                ).astype(BF16)
+            weight_terms(turned, dec_cot, dec_dw, channels)
             turn(enc_act)
+            scatter_start(p, c, sibling, dec_dw, dec_sibling, dec_pair, dec_chips, dec_sems)
 
         j_eb, enc_bwd = window((4 * sections - 2 - own) * PACE)
 
@@ -308,7 +426,8 @@
             upstream = fwd_sum(bwd_in[micros + j], scot_in[j])
             keep = keep_ref[j, own].astype(F32)
             taps = spatial_taps(keep * upstream, -1)
-            cot = cube(transposed_product(taps, enc_w, channels)[:24])
+            columns = jnp.concatenate(taps, axis=1)
+            cot = cube(jnp.dot(columns, enc_w[...], preferred_element_type=F32)[:24])
             grad, gain_part = norm_backward(
                 cot, enc_normed[j], enc_scale[j], enc_slope[j], enc_gain_ref[...], mix_ref, count
             )
@@ -319,7 +438,7 @@
                 send(q_out, j, bwd_in, micros + j, bwd_sem, 5, before).start()
 
             dge_ref[...] += gain_part
-            enc_cot[pl.ds(pl.multiple_of(j * 32, 32), 32), :] = jnp.concatenate(taps, axis=1)
+            enc_cot[pl.ds(pl.multiple_of(j * 32, 32), 32), :] = columns
 
         return carry
 
@@ -327,12 +446,53 @@
         return cube((stream.astype(F32) + skip.astype(F32)).astype(BF16).astype(F32))
 
     lax.fori_loop(0, (4 * sections - 2) * PACE + micros, step, 0)
-    for tap in range(9):
-        dwe_ref[tap * channels : (tap + 1) * channels, :] = jnp.dot(
-            turned[...],
-            enc_cot[:, tap * channels : (tap + 1) * channels],
-            preferred_element_type=F32,
-        ).astype(BF16)
+    row = lax.broadcasted_iota(jnp.int32, (8, channels), 0)
+    gain_own[...] = jnp.where(
+        row == 0,
+        jnp.sum(dge_ref[...], axis=0, keepdims=True),
+        jnp.where(row == 1, jnp.sum(dgd_ref[...], axis=0, keepdims=True), 0.0),
+    )
+    to_pair = pltpu.make_async_remote_copy(
+        src_ref=gain_own,
+        dst_ref=gain_sibling,
+        send_sem=gain_pair_sem.at[0],
+        recv_sem=gain_pair_sem.at[1],
+        device_id={"dp": sibling},
+        device_id_type=MESH,
+    )
+    to_pair.start()
+    weight_terms(turned, enc_cot, enc_dw, channels)
+    scatter_start(p, c, sibling, enc_dw, enc_sibling, enc_pair, enc_chips, enc_sems)
+    to_pair.wait()
+    gain_pair[...] = gain_own[...] + gain_sibling[...]
+
+    def gain_to_chip(o, carry):
+        pltpu.make_async_remote_copy(
+            src_ref=gain_pair,
+            dst_ref=gain_chips.at[o - 1],
+            send_sem=gain_chip_sem.at[0, o - 1],
+            recv_sem=gain_chip_sem.at[1, o - 1],
+            device_id={"dp": 2 * lax.rem(p + o, chips) + c},
+            device_id_type=MESH,
+        ).start()
+        return carry
+
+    lax.fori_loop(1, chips, gain_to_chip, 0)
+    scatter_end(p, c, dec_dw, dec_sibling, dec_pair, dec_chips, dec_sems, dwd_out)
+    scatter_end(p, c, enc_dw, enc_sibling, enc_pair, enc_chips, enc_sems, dwe_out)
+
+    def gain_arrived(o, carry):
+        for side in range(2):
+            pltpu.make_async_copy(
+                gain_chips.at[o], gain_chips.at[o], gain_chip_sem.at[side, o]
+            ).wait()
+        return carry
+
+    lax.fori_loop(0, chips - 1, gain_arrived, 0)
+    total = gain_pair[...]
+    for o in range(chips - 1):
+        total = total + gain_chips[o]
+    gain_out[...] = total
 
     def drain(j, carry):
         for kind, source in ((0, enc_out), (1, enc_out), (3, g_out), (4, s_out)):
@@ -382,18 +542,23 @@
     slots = lambda n: pltpu.VMEM((n, positions, channels), BF16)
     kept = lambda: pltpu.VMEM((micros, 3, 8, channels), F32)
     rows = 32 * micros
-    dwe, dwd, dge, dgd = pl.pallas_call(
+    group = lax.axis_size("dp")
+    chips = group // 2
+    wide = lambda *lead: pltpu.VMEM(lead + (40, channels), BF16)
+    enc_blocks, dec_blocks = 9 * channels // group // 40, 3 * channels // group // 40
+    shares = lambda n: [wide(chips, 2, n), wide(chips, n), wide(chips, n), wide(chips - 1, n)]
+    dwe, dwd, gains = pl.pallas_call(
         lambda *refs: pipeline_kernel(sections, micros, scale, *refs),
         out_shape=(
-            jax.ShapeDtypeStruct((9 * channels, channels), BF16),
-            jax.ShapeDtypeStruct((3 * channels, channels), BF16),
-            jax.ShapeDtypeStruct((8, channels), F32),
+            jax.ShapeDtypeStruct((enc_blocks, 40, channels), F32),
+            jax.ShapeDtypeStruct((dec_blocks, 40, channels), F32),
             jax.ShapeDtypeStruct((8, channels), F32),
         ),
         in_specs=[pl.BlockSpec(memory_space=pltpu.SMEM), vmem, vmem, vmem, vmem, vmem, hbm, hbm],
-        out_specs=(vmem, vmem, vmem, vmem),
+        out_specs=(vmem, vmem, vmem),
         scratch_shapes=[
             pltpu.VMEM((9 * channels, channels), BF16),
+            pltpu.VMEM((3 * channels, channels), BF16),
             pltpu.VMEM((3 * channels, channels), BF16),
             slots(2 * micros),
             slots(2 * micros),
@@ -415,24 +580,40 @@
             pltpu.VMEM((rows, 9 * channels), BF16),
             pltpu.VMEM((rows, 3 * channels), BF16),
             pltpu.VMEM((channels, rows), BF16),
+            pltpu.VMEM((8, channels), F32),
+            pltpu.VMEM((8, channels), F32),
+            pltpu.VMEM((8, channels), F32),
+            pltpu.VMEM((8, channels), F32),
+            pltpu.VMEM((8, channels), F32),
+            pltpu.VMEM((chips - 1, 8, channels), F32),
+            *shares(enc_blocks),
+            *shares(dec_blocks),
             pltpu.SemaphoreType.DMA((2,)),
             pltpu.SemaphoreType.DMA((2 * micros,)),
             pltpu.SemaphoreType.DMA((2 * micros,)),
             pltpu.SemaphoreType.DMA((micros,)),
             pltpu.SemaphoreType.DMA((micros,)),
             pltpu.SemaphoreType.DMA((6, micros)),
+            pltpu.SemaphoreType.DMA((2, chips)),
+            pltpu.SemaphoreType.DMA((2, chips - 1)),
+            pltpu.SemaphoreType.DMA((2, chips)),
+            pltpu.SemaphoreType.DMA((2, chips - 1)),
+            pltpu.SemaphoreType.DMA((2,)),
+            pltpu.SemaphoreType.DMA((2, chips - 1)),
         ],
         compiler_params=pltpu.CompilerParams(
-            collective_id=0, has_side_effects=True, vmem_limit_bytes=56 << 20
+            collective_id=0, has_side_effects=True, vmem_limit_bytes=60 << 20
         ),
         name="pipeline",
     )(keep_lists, first, noise, enc_gain, dec_gain, mix, enc_weight[0], dec_weight[0])
-    gains = jnp.stack([jnp.sum(dge, axis=0), jnp.sum(dgd, axis=0)]).astype(BF16)
-    scatter = lambda value, dim: lax.psum_scatter(
-        value, "dp", scatter_dimension=dim, tiled=True
-    ).astype(F32)
-    dwe, dwd, gains = scatter(dwe, 0), scatter(dwd, 0), scatter(gains, 1)
-    return (dwe[None], gains[:1], dwd[None], gains[1:])
+    part = channels // group
+    gains = lax.dynamic_slice_in_dim(gains, lax.axis_index("dp") * part, part, 1)
+    return (
+        dwe.reshape(1, -1, channels),
+        gains[0:1],
+        dwd.reshape(1, -1, channels),
+        gains[1:2],
+    )
 
 
 def solution(mesh):

time: 559 us -> 413 us (0.74)
  waiting for transfers between devices: 122 us -> 0 us
  blocking collectives: 80.1 us -> 0 us
  Pallas kernels: 332 us -> 402 us
  between operations: 14.8 us -> 0.7 us
    unnamed x4 -> x0, waiting for transfers between devices: 122 us -> none
    unnamed x1 -> x0, blocking collectives: 80.1 us -> none
    pallas_call x1, Pallas kernels: 332 us -> 402 us  [body(): pl.pallas_call(lambda *refs: pipeline_kernel(sections, micros, scale, *re...]
  transfers between devices with their start and end apart: 2 -> 0, of which waited for: 2 -> 0; matrix products, arithmetic and copies ran while one was open for 1% -> 0% of each run, Pallas kernels for 0% -> 0%
where the time goes in v2:
time: 413 us
  Pallas kernels  402 us (97%)
  local copies, waits for them, and re-layouts  6.38 us (2%)
    pallas_call x1, Pallas kernels, body(): pl.pallas_call(lambda *refs: pipeline_kernel(sections, micros, scale, *re...  402 us

profile of v2, /device:TPU:1, one launch (start us, length us, event | category | flops | bytes accessed | tf_op | source)
XLA Modules:
  0.0 412.6 jit_solution(8954043114083162891)
XLA Ops:
  0.6 0.9 slice_convert_fusion.3
  1.7 0.7 broadcast_compare_fusion.3
  2.4 1.0 reshape.67.refs_2_
  3.4 0.0 copy-start
  3.4 0.7 fusion
  4.2 1.0 add_convert_fusion.refs_1_
  5.2 0.0 copy-done
  5.2 402.2 %pipeline.1 = (f32[9,40,640]{2,1,0:T(8,128)}, f32[3,40,640]{2,1,0:T(8,128)}, f32[8,640]{1,0:T(8,128)}) custom-call(s32[8,32]{1,0:T(8,128)} %refs_0_.1, bf16[8,24,640]{2,1,0:T(8,128)(2,1)} %add_convert_fusion.refs_1_, bf16[8,24,640]{2,1,0:T(8,128)(2,1)} %copy-done, f32[1,640]{1,0:T(1,128)} %refs_3_.1, f32[1,640]{1,0:T(1,128)} %refs_4_.1, ...), custom_call_target="tpu_custom_call" | custom-call | tf_op jit(solution)/shard_map/pipeline/pallas_call | solution.py:550
  407.4 0.8 constant_dynamic-slice_fusion
  408.2 0.5 fusion.1
  408.7 2.2 copy.16
  410.9 1.7 copy.17
  (4 shorter events, 0.2 us)
Async XLA Ops:
  3.4 1.8 copy-start

commit v3 on v2

v3 whole, which is shorter than its diff:
```python
import math

import jax
import jax.numpy as jnp
import numpy as np
from jax import lax
from jax.experimental import pallas as pl
from jax.experimental.pallas import tpu as pltpu
from jax.sharding import PartitionSpec as P

GROUPS = 32
F32, BF16 = jnp.float32, jnp.bfloat16
MESH = pl.DeviceIdType.MESH


def noise_level(timesteps):
    phase_arg = (timesteps.astype(F32) / 1000.0 + 0.008) / 1.008
    return jnp.cos(phase_arg * (math.pi / 2.0)) ** 2


def over_rows(values):
    part = values[:, 0] + values[:, 1] + values[:, 2]
    return jnp.broadcast_to(jnp.sum(part, axis=1, keepdims=True), part.shape)


def split_terms(values):
    high = values.astype(BF16).astype(F32)
    rest = values - high
    middle = rest.astype(BF16).astype(F32)
    return [high, middle, rest - middle]


def group_means(sums, mix_ref, count):
    terms = [term for each in sums for term in split_terms(each)]
    stacked = jnp.concatenate(terms, axis=0)
    samples, rows, channels = sums[0].shape
    mixed = jnp.dot(
        stacked.reshape(-1, channels).astype(BF16), mix_ref[...], preferred_element_type=F32
    ).reshape(-1, samples, rows, channels)
    return [
        (mixed[3 * i] + mixed[3 * i + 1] + mixed[3 * i + 2]) * (1.0 / count)
        for i in range(len(sums))
    ]


def cube(values):
    return values.reshape(-1, 3, 8, values.shape[-1])


def uncube(product):
    return product.reshape(-1, 4, 8, product.shape[-1])[:, :3]


def flat(values):
    return values.reshape(-1, 24, values.shape[-1]).astype(BF16)


def padded_rows(values):
    full = jnp.concatenate([values, jnp.zeros_like(values[:, :1])], axis=1)
    return full.reshape(-1, values.shape[-1]).astype(BF16)


def spatial_taps(values, sign):
    place = lax.broadcasted_iota(jnp.int32, values.shape, 2)
    high, wide = place // 2, place % 2
    taps = []
    for tap in range(9):
        down, across = sign * (tap // 3 - 1), sign * (tap % 3 - 1)
        shift = 2 * down + across
        moved = pltpu.roll(values, (-shift) % 8, 2) if shift % 8 else values
        if down or across:
            inside = (
                (high + down >= 0) & (high + down < 4) & (wide + across >= 0) & (wide + across < 2)
            )
            moved = jnp.where(inside, moved, 0.0)
        taps.append(padded_rows(moved))
    return jnp.concatenate(taps, axis=1)


def temporal_taps(values, sign):
    zero = jnp.zeros_like(values[:, :1])
    before = jnp.concatenate([zero, values[:, :2]], axis=1)
    after = jnp.concatenate([values[:, 1:], zero], axis=1)
    taps = [before, values, after] if sign > 0 else [after, values, before]
    return jnp.concatenate([padded_rows(tap) for tap in taps], axis=1)


def norm_forward(values, gain, mix_ref, count):
    mean = group_means([over_rows(values)], mix_ref, count)[0]
    center = values - mean[:, None]
    spread = group_means([over_rows(center * center)], mix_ref, count)[0]
    scale = lax.rsqrt(spread + 1e-05)
    normed = center * scale[:, None]
    z = normed * gain[None, None]
    gate = 1.0 / (1.0 + jnp.exp(-z))
    return normed, scale, z, gate


def norm_backward(cot, normed, scale, slope, gain, mix_ref, count):
    dz = cot * slope
    gain_part = dz * normed
    gain_part = jnp.sum(gain_part[:, 0] + gain_part[:, 1] + gain_part[:, 2], axis=0)
    dn = dz * gain[None, None]
    mean_dn, mean_dnn = group_means([over_rows(dn), over_rows(dn * normed)], mix_ref, count)
    grad = scale[:, None] * (dn - mean_dn[:, None] - normed * mean_dnn[:, None])
    return grad, gain_part


def gated(values, keeps):
    return jnp.concatenate([values[s : s + 1] * keep for s, keep in enumerate(keeps)], axis=0)


def transposed_product(columns, weight_ref, channels):
    total = None
    for at in range(0, columns.shape[1], channels):
        part = lax.dot_general(
            columns[:, at : at + channels],
            weight_ref[at : at + channels, :],
            (((1,), (1,)), ((), ())),
            preferred_element_type=F32,
        )
        total = part if total is None else total + part
    return total


def scatter_start(p, c, sibling, dw, from_sibling, pair, from_chips, sems):
    chips = dw.shape[0]
    send_pair, arrive_pair, send_chip, arrive_chip = sems

    def to_sibling(o, carry):
        m = lax.rem(p + o, chips)
        pltpu.make_async_remote_copy(
            src_ref=dw.at[m, 1 - c],
            dst_ref=from_sibling.at[m],
            send_sem=send_pair.at[m],
            recv_sem=arrive_pair.at[m],
            device_id={"dp": sibling},
            device_id_type=MESH,
        ).start()
        return carry

    def to_chip(o, carry):
        m = lax.rem(p + o, chips)
        pltpu.make_async_copy(from_sibling.at[m], from_sibling.at[m], arrive_pair.at[m]).wait()

        def add(block, inner):
            pair[m, block] = (
                dw[m, c, block].astype(F32) + from_sibling[m, block].astype(F32)
            ).astype(BF16)
            return inner

        lax.fori_loop(0, dw.shape[2], add, 0)
        pltpu.make_async_remote_copy(
            src_ref=pair.at[m],
            dst_ref=from_chips.at[o - 1],
            send_sem=send_chip.at[o - 1],
            recv_sem=arrive_chip.at[o - 1],
            device_id={"dp": 2 * m + c},
            device_id_type=MESH,
        ).start()
        return carry

    lax.fori_loop(1, chips + 1, to_sibling, 0)
    lax.fori_loop(1, chips, to_chip, 0)
    pltpu.make_async_copy(from_sibling.at[p], from_sibling.at[p], arrive_pair.at[p]).wait()


def scatter_end(p, c, dw, from_sibling, pair, from_chips, sems, out_ref):
    chips = dw.shape[0]
    send_pair, arrive_pair, send_chip, arrive_chip = sems

    def arrive(o, carry):
        pltpu.make_async_copy(from_chips.at[o], from_chips.at[o], arrive_chip.at[o]).wait()
        return carry

    def add(block, carry):
        total = dw[p, c, block].astype(F32) + from_sibling[p, block].astype(F32)
        for o in range(chips - 1):
            total = total + from_chips[o, block].astype(F32)
        out_ref[block] = total
        return carry

    def sent(o, carry):
        pltpu.make_async_copy(pair.at[o], pair.at[o], send_chip.at[o]).wait()
        return carry

    def sent_pair(m, carry):
        pltpu.make_async_copy(from_sibling.at[m], from_sibling.at[m], send_pair.at[m]).wait()
        return carry

    lax.fori_loop(0, chips - 1, arrive, 0)
    lax.fori_loop(0, dw.shape[2], add, 0)
    lax.fori_loop(0, chips - 1, sent, 0)
    lax.fori_loop(0, chips, sent_pair, 0)


def weight_terms(turned, cot, dw, channels):
    blocks = dw.shape[2]
    for tap in range(cot.shape[1] // channels):
        part = jnp.dot(
            turned,
            cot[:, tap * channels : (tap + 1) * channels],
            preferred_element_type=F32,
        ).reshape(channels // 40, 40, channels)
        for i in range(channels // 40):
            at = tap * (channels // 40) + i
            dw[at // (2 * blocks), (at // blocks) % 2, at % blocks] = part[i].astype(BF16)


def pipeline_kernel(
    sections,
    micros,
    loss_scale,
    keep_ref,
    first_ref,
    noise_ref,
    enc_gain_ref,
    dec_gain_ref,
    mix_ref,
    enc_hbm,
    dec_hbm,
    dwe_out,
    dwd_out,
    gain_out,
    enc_w,
    dec_w,
    gain_quad,
    fwd_in,
    bwd_in,
    skip_in,
    scot_in,
    dec_in,
    grad_in,
    enc_out,
    dec_out,
    grad_out,
    s_out,
    q_out,
    enc_normed,
    enc_slope,
    enc_scale,
    enc_act,
    enc_cot,
    dec_normed,
    dec_slope,
    dec_scale,
    act_out,
    h_out,
    part_out,
    act_in,
    h_in,
    part_in,
    dec_act,
    dec_cot,
    turned,
    dge_ref,
    gain_own,
    gain_pair,
    gain_sibling,
    gain_chips,
    enc_dw,
    enc_sibling,
    enc_pair,
    enc_chips,
    dec_dw,
    dec_sibling,
    dec_pair,
    dec_chips,
    local_sem,
    quad_send,
    quad_sem,
    half_send,
    half_sem,
    fwd_sem,
    bwd_sem,
    skip_sem,
    scot_sem,
    dec_sem,
    grad_sem,
    owner_send,
    owner_sem,
    enc_send,
    dec_send,
    enc_pair_sem,
    enc_chip_sem,
    dec_pair_sem,
    dec_chip_sem,
    gain_pair_sem,
    gain_chip_sem,
):
    channels = noise_ref.shape[-1]
    count = 24 * (channels // GROUPS)
    own = lax.axis_index("section")
    last = sections - 1
    quad, member = own // 4, lax.rem(own, 4)
    quads = sections // 4
    dp = lax.axis_index("dp")
    p, c = dp // 2, lax.rem(dp, 2)
    sibling = dp + 1 - 2 * c
    chips = enc_dw.shape[0]
    half_rows = dec_w.shape[1] // 2
    enc_sems = [enc_pair_sem.at[0], enc_pair_sem.at[1], enc_chip_sem.at[0], enc_chip_sem.at[1]]
    dec_sems = [dec_pair_sem.at[0], dec_pair_sem.at[1], dec_chip_sem.at[0], dec_chip_sem.at[1]]

    def remote(src, dst, send_sem, recv_sem, **device):
        return pltpu.make_async_remote_copy(
            src_ref=src,
            dst_ref=dst,
            send_sem=send_sem,
            recv_sem=recv_sem,
            device_id=device,
            device_id_type=MESH,
        )

    def wait(ref, sem):
        pltpu.make_async_copy(ref, ref, sem).wait()

    load_enc = pltpu.make_async_copy(enc_hbm, enc_w, local_sem.at[0])
    load_dec = pltpu.make_async_copy(dec_hbm, dec_w.at[member], local_sem.at[1])
    load_enc.start()
    load_dec.start()
    gain_quad[member] = jnp.broadcast_to(dec_gain_ref[...], gain_quad.shape[1:])

    barrier = pltpu.get_barrier_semaphore()

    def greet(o, carry):
        pl.semaphore_signal(
            barrier,
            inc=1,
            device_id={"section": lax.rem(own + o, sections)},
            device_id_type=MESH,
        )
        return carry

    lax.fori_loop(1, sections, greet, 0)
    pl.semaphore_signal(barrier, inc=1, device_id={"dp": sibling}, device_id_type=MESH)
    for o in range(1, chips):
        pl.semaphore_signal(
            barrier,
            inc=1,
            device_id={"dp": 2 * lax.rem(p + o, chips) + c},
            device_id_type=MESH,
        )
    pl.semaphore_wait(barrier, last + chips)

    @pl.when(own == 0)
    def _():
        for j in range(micros):
            fwd_in[j] = first_ref[j]

    half = pl.ds(pl.multiple_of(c * half_rows, half_rows), half_rows)
    other_half = pl.ds(pl.multiple_of((1 - c) * half_rows, half_rows), half_rows)

    def share(o, carry):
        to = 4 * quad + lax.rem(member + o, 4)
        remote(
            dec_hbm.at[half],
            dec_w.at[member, half],
            quad_send.at[0, o],
            quad_sem.at[0, member],
            section=to,
        ).start()
        remote(
            gain_quad.at[member],
            gain_quad.at[member],
            quad_send.at[1, o],
            quad_sem.at[1, member],
            section=to,
        ).start()
        return carry

    lax.fori_loop(1, 4, share, 0)
    dge_ref[...] = jnp.zeros_like(dge_ref)
    load_enc.wait()

    opposite = last - own
    opposite_quad, opposite_level = opposite // 4, lax.rem(opposite, 4)

    def enc_forward(j, carry):
        @pl.when(own > 0)
        def _():
            wait(fwd_in.at[j], fwd_sem.at[j])

        values = cube(fwd_in[j].astype(F32))
        keep = keep_ref[j, own].astype(F32)
        normed, scale, z, gate = norm_forward(values, enc_gain_ref[...], mix_ref, count)
        act = z * gate
        columns = spatial_taps(act, 1)
        branch = uncube(jnp.dot(columns, enc_w[...], preferred_element_type=F32))
        enc_out[j] = flat(values + keep * branch)[0]

        @pl.when(own < last)
        def _():
            remote(
                enc_out.at[j], fwd_in.at[j], enc_send.at[0, j], fwd_sem.at[j], section=own + 1
            ).start()

        pair, side = j // 2, lax.rem(j, 2)

        @pl.when(own == last)
        def _():
            remote(
                enc_out.at[j], dec_in.at[side], enc_send.at[0, j], dec_sem.at[side], section=pair
            ).start()

        remote(
            enc_out.at[j],
            skip_in.at[opposite_level, side],
            enc_send.at[1, j],
            skip_sem.at[opposite_level, side],
            section=4 * opposite_quad + pair,
        ).start()
        enc_normed[j] = normed[0]
        enc_scale[j] = scale[0]
        enc_slope[j] = (gate * (1.0 + z * (1.0 - gate)))[0]
        enc_act[pl.ds(pl.multiple_of(j * 32, 32), 32), :] = padded_rows(act)
        return carry

    lax.fori_loop(0, micros, enc_forward, 0)

    def turn_tap(tap, carry):
        rows = pl.ds(pl.multiple_of(tap * channels, channels), channels)
        enc_w[rows, :] = enc_w[rows, :].astype(F32).T.astype(BF16)
        return carry

    def pass_half(o, carry):
        of = lax.rem(member + o, 4)
        wait(dec_w.at[of, half], quad_sem.at[0, of])
        wait(gain_quad.at[of], quad_sem.at[1, of])
        remote(
            dec_w.at[of, half], dec_w.at[of, half], half_send.at[of], half_sem.at[of], dp=sibling
        ).start()
        return carry

    def take_half(o, carry):
        of = lax.rem(member + o, 4)
        wait(dec_w.at[of, other_half], half_sem.at[of])
        return carry

    load_dec.wait()
    lax.fori_loop(1, 4, pass_half, 0)
    lax.fori_loop(0, 9, turn_tap, 0)
    turned[...] = enc_act[...].astype(F32).T.astype(BF16)
    lax.fori_loop(1, 4, take_half, 0)

    mine = pl.ds(2 * member, 2)

    @pl.when(quad == 0)
    def _():
        for side in range(2):
            wait(dec_in.at[side], dec_sem.at[side])

    @pl.when(quad > 0)
    def _():
        wait(dec_in, dec_sem.at[2])

    def dec_keeps(level):
        return [
            keep_ref[2 * member + side, sections + 4 * quad + level].astype(F32)
            for side in range(2)
        ]

    def to_owner(source, target, kind, level):
        @pl.when(level != member)
        def _():
            remote(
                source.at[level],
                target,
                owner_send.at[kind, level],
                owner_sem.at[kind, member],
                section=4 * quad + level,
            ).start()

    def dec_forward(level, stream):
        for side in range(2):
            wait(skip_in.at[level, side], skip_sem.at[level, side])
        values = stream + cube(skip_in[level].astype(F32))
        normed, scale, z, gate = norm_forward(values, gain_quad[level], mix_ref, count)
        act = z * gate
        branch = uncube(
            jnp.dot(temporal_taps(act, 1), dec_w[level], preferred_element_type=F32)
        )
        result = (stream + gated(branch, dec_keeps(level))).astype(BF16).astype(F32)
        dec_normed[level] = normed
        dec_scale[level] = scale
        dec_slope[level] = gate * (1.0 + z * (1.0 - gate))
        act_out[level] = flat(act)
        to_owner(act_out, act_in.at[mine], 0, level)
        return result

    result = lax.fori_loop(0, 4, dec_forward, cube(dec_in[...].astype(F32)))

    @pl.when(quad < quads - 1)
    def _():
        dec_out[...] = flat(result)
        remote(dec_out, dec_in, dec_send.at[0], dec_sem.at[2], section=own + 4).start()
        wait(grad_in, grad_sem)

    @pl.when(quad == quads - 1)
    def _():
        gap = result - cube(noise_ref[mine].astype(F32))
        grad_in[...] = flat(gap * loss_scale)

    def dec_backward(step, upstream):
        level = 3 - step
        gate = gated(upstream, dec_keeps(level))
        h_out[level] = flat(gate)
        to_owner(h_out, h_in.at[mine], 1, level)
        columns = temporal_taps(gate, -1)
        cot = uncube(transposed_product(columns, dec_w.at[level], channels))
        grad, gain_part = norm_backward(
            cot,
            dec_normed[level],
            dec_scale[level],
            dec_slope[level],
            gain_quad[level],
            mix_ref,
            count,
        )
        s_out[level] = flat(grad)
        remote(
            s_out.at[level],
            scot_in.at[mine],
            dec_send.at[2 + level],
            scot_sem.at[member],
            section=last - 4 * quad - level,
        ).start()
        part_out[level] = gain_part
        to_owner(part_out, part_in.at[member], 2, level)
        return (upstream + grad).astype(BF16).astype(F32)

    result = lax.fori_loop(0, 4, dec_backward, cube(grad_in[...].astype(F32)))
    grad_out[...] = flat(result)

    @pl.when(quad > 0)
    def _():
        remote(grad_out, grad_in, dec_send.at[1], grad_sem, section=own - 4).start()

    @pl.when(quad == 0)
    def _():
        remote(
            grad_out, bwd_in.at[mine], dec_send.at[1], bwd_sem.at[micros + member], section=last
        ).start()

    act_in[mine] = act_out[member]
    h_in[mine] = h_out[member]
    part_in[member] = part_out[member]

    def from_member(o, carry):
        of = lax.rem(member + o, 4)
        theirs = pl.ds(2 * of, 2)
        wait(act_in.at[theirs], owner_sem.at[0, of])
        wait(h_in.at[theirs], owner_sem.at[1, of])
        wait(part_in.at[of], owner_sem.at[2, of])
        return carry

    lax.fori_loop(1, 4, from_member, 0)

    def lay_out(j, carry):
        rows = pl.ds(pl.multiple_of(j * 32, 32), 32)
        dec_act[rows, :] = padded_rows(cube(act_in[j].astype(F32)))
        dec_cot[rows, :] = temporal_taps(cube(h_in[j].astype(F32)), -1)
        return carry

    lax.fori_loop(0, micros, lay_out, 0)
    weight_terms(dec_act[...].astype(F32).T.astype(BF16), dec_cot, dec_dw, channels)
    scatter_start(p, c, sibling, dec_dw, dec_sibling, dec_pair, dec_chips, dec_sems)

    def enc_backward(j, carry):
        @pl.when(lax.rem(j, 2) == 0)
        def _():
            pair = j // 2
            both = pl.ds(j, 2)
            wait(scot_in.at[both], scot_sem.at[pair])

            @pl.when(own == last)
            def _():
                wait(bwd_in.at[both], bwd_sem.at[micros + pair])

        @pl.when(own < last)
        def _():
            wait(bwd_in.at[j], bwd_sem.at[j])

        upstream = cube(
            (bwd_in[j].astype(F32) + scot_in[j].astype(F32)).astype(BF16).astype(F32)
        )
        keep = keep_ref[j, own].astype(F32)
        columns = spatial_taps(keep * upstream, -1)
        cot = uncube(jnp.dot(columns, enc_w[...], preferred_element_type=F32))
        grad, gain_part = norm_backward(
            cot,
            enc_normed[j][None],
            enc_scale[j][None],
            enc_slope[j][None],
            enc_gain_ref[...],
            mix_ref,
            count,
        )

        @pl.when(own > 0)
        def _():
            q_out[j] = flat(upstream + grad)[0]
            remote(
                q_out.at[j], bwd_in.at[j], enc_send.at[2, j], bwd_sem.at[j], section=own - 1
            ).start()

        dge_ref[...] += gain_part
        enc_cot[pl.ds(pl.multiple_of(j * 32, 32), 32), :] = columns
        return carry

    lax.fori_loop(0, micros, enc_backward, 0)
    dgd = part_in[0] + part_in[1] + part_in[2] + part_in[3]
    row = lax.broadcasted_iota(jnp.int32, (8, channels), 0)
    gain_own[...] = jnp.where(
        row == 0,
        jnp.sum(dge_ref[...], axis=0, keepdims=True),
        jnp.where(row == 1, jnp.sum(dgd, axis=0, keepdims=True), 0.0),
    )
    to_pair = remote(
        gain_own, gain_sibling, gain_pair_sem.at[0], gain_pair_sem.at[1], dp=sibling
    )
    to_pair.start()
    weight_terms(turned[...], enc_cot, enc_dw, channels)
    scatter_start(p, c, sibling, enc_dw, enc_sibling, enc_pair, enc_chips, enc_sems)
    to_pair.wait()
    gain_pair[...] = gain_own[...] + gain_sibling[...]

    def gain_to_chip(o, carry):
        remote(
            gain_pair,
            gain_chips.at[o - 1],
            gain_chip_sem.at[0, o - 1],
            gain_chip_sem.at[1, o - 1],
            dp=2 * lax.rem(p + o, chips) + c,
        ).start()
        return carry

    lax.fori_loop(1, chips, gain_to_chip, 0)
    scatter_end(p, c, dec_dw, dec_sibling, dec_pair, dec_chips, dec_sems, dwd_out)
    scatter_end(p, c, enc_dw, enc_sibling, enc_pair, enc_chips, enc_sems, dwe_out)

    def gain_arrived(o, carry):
        for side in range(2):
            wait(gain_chips.at[o], gain_chip_sem.at[side, o])
        return carry

    lax.fori_loop(0, chips - 1, gain_arrived, 0)
    total = gain_pair[...]
    for o in range(chips - 1):
        total = total + gain_chips[o]
    gain_out[...] = total

    def drain(j, carry):
        for kind in range(2):
            wait(enc_out.at[j], enc_send.at[kind, j])

        @pl.when(own > 0)
        def _():
            wait(q_out.at[j], enc_send.at[2, j])

        return carry

    def drain_quad(o, carry):
        of = lax.rem(member + o, 4)
        wait(dec_w.at[of, half], quad_send.at[0, o])
        wait(gain_quad.at[of], quad_send.at[1, o])
        wait(dec_w.at[of, half], half_send.at[of])
        wait(act_out.at[of], owner_send.at[0, of])
        wait(h_out.at[of], owner_send.at[1, of])
        wait(part_out.at[of], owner_send.at[2, of])
        return carry

    def drain_scot(level, carry):
        wait(s_out.at[level], dec_send.at[2 + level])
        return carry

    lax.fori_loop(0, micros, drain, 0)
    lax.fori_loop(1, 4, drain_quad, 0)
    lax.fori_loop(0, 4, drain_scot, 0)
    wait(grad_out, dec_send.at[1])

    @pl.when(quad < quads - 1)
    def _():
        wait(dec_out, dec_send.at[0])


def body(
    clip_pool,
    sample_ids,
    timesteps,
    noise_draw,
    keep_lists,
    enc_weight,
    enc_gain,
    dec_weight,
    dec_gain,
):
    sections = lax.axis_size("section")
    micros = noise_draw.shape[0]
    channels = noise_draw.shape[-1]
    positions = noise_draw.shape[1] * noise_draw.shape[2] * noise_draw.shape[3]
    scale = 1.0 / math.sqrt(micros * lax.axis_size("dp") * positions)
    lined = (micros, positions, channels)
    noise = noise_draw.reshape(lined)
    clips = clip_pool.reshape((-1,) + lined[1:])
    clean = jnp.zeros(lined, F32)
    for clip in range(clips.shape[0]):
        clean = jnp.where((sample_ids == clip)[:, None, None], clips[clip][None].astype(F32), clean)
    level = noise_level(timesteps)[:, None, None]
    first = (jnp.sqrt(level) * clean + jnp.sqrt(1.0 - level) * noise.astype(F32)).astype(BF16)
    member = np.arange(channels) // (channels // GROUPS)
    mix = jnp.asarray((member[:, None] == member[None, :]).astype(np.float32), BF16)
    vmem = pl.BlockSpec(memory_space=pltpu.VMEM)
    hbm = pl.BlockSpec(memory_space=pl.ANY)
    slots = lambda *lead: pltpu.VMEM(lead + (positions, channels), BF16)
    kept = lambda *lead: pltpu.VMEM(lead + (3, 8, channels), F32)
    rows = 32 * micros
    group = lax.axis_size("dp")
    chips = group // 2
    wide = lambda *lead: pltpu.VMEM(lead + (40, channels), BF16)
    enc_blocks, dec_blocks = 9 * channels // group // 40, 3 * channels // group // 40
    shares = lambda n: [wide(chips, 2, n), wide(chips, n), wide(chips, n), wide(chips - 1, n)]
    dwe, dwd, gains = pl.pallas_call(
        lambda *refs: pipeline_kernel(sections, micros, scale, *refs),
        out_shape=(
            jax.ShapeDtypeStruct((enc_blocks, 40, channels), F32),
            jax.ShapeDtypeStruct((dec_blocks, 40, channels), F32),
            jax.ShapeDtypeStruct((8, channels), F32),
        ),
        in_specs=[pl.BlockSpec(memory_space=pltpu.SMEM), vmem, vmem, vmem, vmem, vmem, hbm, hbm],
        out_specs=(vmem, vmem, vmem),
        scratch_shapes=[
            pltpu.VMEM((9 * channels, channels), BF16),
            pltpu.VMEM((4, 3 * channels, channels), BF16),
            pltpu.VMEM((4, 8, channels), F32),
            slots(micros),
            slots(micros),
            slots(4, 2),
            slots(micros),
            slots(2),
            slots(2),
            slots(micros),
            slots(2),
            slots(2),
            slots(4, 2),
            slots(micros),
            kept(micros),
            kept(micros),
            pltpu.VMEM((micros, 8, channels), F32),
            pltpu.VMEM((rows, channels), BF16),
            pltpu.VMEM((rows, 9 * channels), BF16),
            kept(4, 2),
            kept(4, 2),
            pltpu.VMEM((4, 2, 8, channels), F32),
            slots(4, 2),
            slots(4, 2),
            pltpu.VMEM((4, 8, channels), F32),
            slots(micros),
            slots(micros),
            pltpu.VMEM((4, 8, channels), F32),
            pltpu.VMEM((rows, channels), BF16),
            pltpu.VMEM((rows, 3 * channels), BF16),
            pltpu.VMEM((channels, rows), BF16),
            pltpu.VMEM((8, channels), F32),
            pltpu.VMEM((8, channels), F32),
            pltpu.VMEM((8, channels), F32),
            pltpu.VMEM((8, channels), F32),
            pltpu.VMEM((chips - 1, 8, channels), F32),
            *shares(enc_blocks),
            *shares(dec_blocks),
            pltpu.SemaphoreType.DMA((2,)),
            pltpu.SemaphoreType.DMA((2, 4)),
            pltpu.SemaphoreType.DMA((2, 4)),
            pltpu.SemaphoreType.DMA((4,)),
            pltpu.SemaphoreType.DMA((4,)),
            pltpu.SemaphoreType.DMA((micros,)),
            pltpu.SemaphoreType.DMA((micros + 4,)),
            pltpu.SemaphoreType.DMA((4, 2)),
            pltpu.SemaphoreType.DMA((4,)),
            pltpu.SemaphoreType.DMA((3,)),
            pltpu.SemaphoreType.DMA,
            pltpu.SemaphoreType.DMA((3, 4)),
            pltpu.SemaphoreType.DMA((3, 4)),
            pltpu.SemaphoreType.DMA((3, micros)),
            pltpu.SemaphoreType.DMA((6,)),
            pltpu.SemaphoreType.DMA((2, chips)),
            pltpu.SemaphoreType.DMA((2, chips - 1)),
            pltpu.SemaphoreType.DMA((2, chips)),
            pltpu.SemaphoreType.DMA((2, chips - 1)),
            pltpu.SemaphoreType.DMA((2,)),
            pltpu.SemaphoreType.DMA((2, chips - 1)),
        ],
        compiler_params=pltpu.CompilerParams(
            collective_id=0, has_side_effects=True, vmem_limit_bytes=60 << 20
        ),
        name="pipeline",
    )(keep_lists, first, noise, enc_gain, dec_gain, mix, enc_weight[0], dec_weight[0])
    part = channels // group
    gains = lax.dynamic_slice_in_dim(gains, lax.axis_index("dp") * part, part, 1)
    return (
        dwe.reshape(1, -1, channels),
        gains[0:1],
        dwd.reshape(1, -1, channels),
        gains[1:2],
    )


def solution(mesh):
    placed = (
        P("dp", None, None, None, None),
        P("dp"),
        P("dp"),
        P("dp", None, None, None, None),
        P("dp", None),
        P("section", None, None),
        P("section", None),
        P("section", None, None),
        P("section", None),
    )
    return jax.shard_map(
        body,
        mesh=mesh,
        in_specs=placed,
        out_specs=(
            P("section", "dp", None),
            P("section", "dp"),
            P("section", "dp", None),
            P("section", "dp"),
        ),
        check_vma=False,
    )
```

time: 413 us -> 384 us (0.930)
  Pallas kernels: 402 us -> 373 us
    pallas_call x1, Pallas kernels: 402 us -> 373 us  [body(): pl.pallas_call(lambda *refs: pipeline_kernel(sections, micros, scale, *re...]
where the time goes in v3:
time: 384 us; the launch traced here: 383 us
  Pallas kernels  373 us (97%)
  local copies, waits for them, and re-layouts  6.38 us (2%)
    pallas_call x1, Pallas kernels, body(): pl.pallas_call(lambda *refs: pipeline_kernel(sections, micros, scale, *re...  373 us

profile of v3, /device:TPU:1, one launch (start us, length us, event | category | flops | bytes accessed | tf_op | source)
XLA Modules:
  0.0 383.5 jit_solution(4011442731999661178)
XLA Ops:
  0.6 0.9 slice_convert_fusion.3
  1.7 0.7 broadcast_compare_fusion.3
  2.4 1.0 reshape.67.refs_2_
  3.4 0.0 copy-start
  3.4 0.7 fusion
  4.2 1.0 add_convert_fusion.refs_1_
  5.2 0.0 copy-done
  5.2 373.1 %pipeline.1 = (f32[9,40,640]{2,1,0:T(8,128)}, f32[3,40,640]{2,1,0:T(8,128)}, f32[8,640]{1,0:T(8,128)}) custom-call(s32[8,32]{1,0:T(8,128)} %refs_0_.1, bf16[8,24,640]{2,1,0:T(8,128)(2,1)} %add_convert_fusion.refs_1_, bf16[8,24,640]{2,1,0:T(8,128)(2,1)} %copy-done, f32[1,640]{1,0:T(1,128)} %refs_3_.1, f32[1,640]{1,0:T(1,128)} %refs_4_.1, ...), custom_call_target="tpu_custom_call" | custom-call | tf_op jit(solution)/shard_map/pipeline/pallas_call | solution.py:723
  378.3 0.8 constant_dynamic-slice_fusion
  379.1 0.5 fusion.1
  379.6 2.2 copy.16
  381.8 1.7 copy.17
  (4 shorter events, 0.2 us)
Async XLA Ops:
  3.4 1.8 copy-start

commit v4 on v3

--- a/solution.py
+++ b/solution.py
@@ -86,9 +86,9 @@
 
 
 def norm_forward(values, gain, mix_ref, count):
-    mean = group_means([over_rows(values)], mix_ref, count)[0]
+    mean, square = group_means([over_rows(values), over_rows(values * values)], mix_ref, count)
+    spread = jnp.maximum(square - mean * mean, 0.0)
     center = values - mean[:, None]
-    spread = group_means([over_rows(center * center)], mix_ref, count)[0]
     scale = lax.rsqrt(spread + 1e-05)
     normed = center * scale[:, None]
     z = normed * gain[None, None]
@@ -224,6 +224,8 @@
     gain_out,
     enc_w,
     dec_w,
+    keep_used,
+    noise_used,
     gain_quad,
     fwd_in,
     bwd_in,
@@ -252,6 +254,7 @@
     part_in,
     dec_act,
     dec_cot,
+    product,
     turned,
     dge_ref,
     gain_own,
@@ -297,6 +300,8 @@
     dp = lax.axis_index("dp")
     p, c = dp // 2, lax.rem(dp, 2)
     sibling = dp + 1 - 2 * c
+    across = 2 - 4 * lax.rem(p, 2)
+    odd = lax.rem(own, 2)
     chips = enc_dw.shape[0]
     half_rows = dec_w.shape[1] // 2
     enc_sems = [enc_pair_sem.at[0], enc_pair_sem.at[1], enc_chip_sem.at[0], enc_chip_sem.at[1]]
@@ -312,6 +317,9 @@
             device_id_type=MESH,
         )
 
+    def at(section):
+        return {"section": section, "dp": dp + across * lax.rem(section + own, 2)}
+
     def wait(ref, sem):
         pltpu.make_async_copy(ref, ref, sem).wait()
 
@@ -327,7 +335,7 @@
         pl.semaphore_signal(
             barrier,
             inc=1,
-            device_id={"section": lax.rem(own + o, sections)},
+            device_id=at(lax.rem(own + o, sections)),
             device_id_type=MESH,
         )
         return carry
@@ -348,6 +356,28 @@
         for j in range(micros):
             fwd_in[j] = first_ref[j]
 
+    @pl.when(odd == 1)
+    def _():
+        remote(keep_ref, keep_used, local_sem.at[2], local_sem.at[3], dp=dp + across).start()
+
+        @pl.when(quad == quads - 1)
+        def _():
+            remote(noise_ref, noise_used, local_sem.at[4], local_sem.at[5], dp=dp + across).start()
+
+        wait(keep_used, local_sem.at[3])
+
+    @pl.when(odd == 0)
+    def _():
+        keep_used[...] = keep_ref[...]
+
+        @pl.when(quad == quads - 1)
+        def _():
+            noise_used[...] = noise_ref[...]
+
+    def kept_at(sample, level):
+        row = keep_used[sample, pl.ds(level, 1), :]
+        return jnp.concatenate([row] * (channels // row.shape[-1]), axis=1)
+
     half = pl.ds(pl.multiple_of(c * half_rows, half_rows), half_rows)
     other_half = pl.ds(pl.multiple_of((1 - c) * half_rows, half_rows), half_rows)
 
@@ -358,18 +388,21 @@
             dec_w.at[member, half],
             quad_send.at[0, o],
             quad_sem.at[0, member],
-            section=to,
+            **at(to),
         ).start()
         remote(
             gain_quad.at[member],
             gain_quad.at[member],
             quad_send.at[1, o],
             quad_sem.at[1, member],
-            section=to,
+            **at(to),
         ).start()
         return carry
 
-    lax.fori_loop(1, 4, share, 0)
+    @pl.when(own >= sections // 2)
+    def _():
+        lax.fori_loop(1, 4, share, 0)
+
     dge_ref[...] = jnp.zeros_like(dge_ref)
     load_enc.wait()
 
@@ -382,7 +415,7 @@
             wait(fwd_in.at[j], fwd_sem.at[j])
 
         values = cube(fwd_in[j].astype(F32))
-        keep = keep_ref[j, own].astype(F32)
+        keep = kept_at(j, own)
         normed, scale, z, gate = norm_forward(values, enc_gain_ref[...], mix_ref, count)
         act = z * gate
         columns = spatial_taps(act, 1)
@@ -392,7 +425,7 @@
         @pl.when(own < last)
         def _():
             remote(
-                enc_out.at[j], fwd_in.at[j], enc_send.at[0, j], fwd_sem.at[j], section=own + 1
+                enc_out.at[j], fwd_in.at[j], enc_send.at[0, j], fwd_sem.at[j], **at(own + 1)
             ).start()
 
         pair, side = j // 2, lax.rem(j, 2)
@@ -400,7 +433,7 @@
         @pl.when(own == last)
         def _():
             remote(
-                enc_out.at[j], dec_in.at[side], enc_send.at[0, j], dec_sem.at[side], section=pair
+                enc_out.at[j], dec_in.at[side], enc_send.at[0, j], dec_sem.at[side], **at(pair)
             ).start()
 
         remote(
@@ -408,7 +441,7 @@
             skip_in.at[opposite_level, side],
             enc_send.at[1, j],
             skip_sem.at[opposite_level, side],
-            section=4 * opposite_quad + pair,
+            **at(4 * opposite_quad + pair),
         ).start()
         enc_normed[j] = normed[0]
         enc_scale[j] = scale[0]
@@ -417,6 +450,10 @@
         return carry
 
     lax.fori_loop(0, micros, enc_forward, 0)
+
+    @pl.when(own < sections // 2)
+    def _():
+        lax.fori_loop(1, 4, share, 0)
 
     def turn_tap(tap, carry):
         rows = pl.ds(pl.multiple_of(tap * channels, channels), channels)
@@ -456,7 +493,7 @@
 
     def dec_keeps(level):
         return [
-            keep_ref[2 * member + side, sections + 4 * quad + level].astype(F32)
+            kept_at(2 * member + side, sections + 4 * quad + level)
             for side in range(2)
         ]
 
@@ -468,7 +505,7 @@
                 target,
                 owner_send.at[kind, level],
                 owner_sem.at[kind, member],
-                section=4 * quad + level,
+                **at(4 * quad + level),
             ).start()
 
     def dec_forward(level, stream):
@@ -490,15 +527,33 @@
 
     result = lax.fori_loop(0, 4, dec_forward, cube(dec_in[...].astype(F32)))
 
+    def halves_left(o, carry):
+        of = lax.rem(member + o, 4)
+        wait(dec_w.at[of, half], half_send.at[of])
+        return carry
+
+    lax.fori_loop(1, 4, halves_left, 0)
+
+    def turn_dec(tap, carry):
+        level = tap // 3
+        rows = pl.ds(pl.multiple_of(lax.rem(tap, 3) * channels, channels), channels)
+        dec_w[level, rows, :] = dec_w[level, rows, :].astype(F32).T.astype(BF16)
+        return carry
+
     @pl.when(quad < quads - 1)
     def _():
         dec_out[...] = flat(result)
-        remote(dec_out, dec_in, dec_send.at[0], dec_sem.at[2], section=own + 4).start()
+        remote(dec_out, dec_in, dec_send.at[0], dec_sem.at[2], **at(own + 4)).start()
+        lax.fori_loop(0, 12, turn_dec, 0)
         wait(grad_in, grad_sem)
 
     @pl.when(quad == quads - 1)
     def _():
-        gap = result - cube(noise_ref[mine].astype(F32))
+        @pl.when(odd == 1)
+        def _():
+            wait(noise_used, local_sem.at[5])
+
+        gap = result - cube(noise_used[mine].astype(F32))
         grad_in[...] = flat(gap * loss_scale)
 
     def dec_backward(step, upstream):
@@ -507,7 +562,16 @@
         h_out[level] = flat(gate)
         to_owner(h_out, h_in.at[mine], 1, level)
         columns = temporal_taps(gate, -1)
-        cot = uncube(transposed_product(columns, dec_w.at[level], channels))
+
+        @pl.when(quad < quads - 1)
+        def _():
+            product[...] = jnp.dot(columns, dec_w[level], preferred_element_type=F32)
+
+        @pl.when(quad == quads - 1)
+        def _():
+            product[...] = transposed_product(columns, dec_w.at[level], channels)
+
+        cot = uncube(product[...])
         grad, gain_part = norm_backward(
             cot,
             dec_normed[level],
@@ -523,7 +587,7 @@
             scot_in.at[mine],
             dec_send.at[2 + level],
             scot_sem.at[member],
-            section=last - 4 * quad - level,
+            **at(last - 4 * quad - level),
         ).start()
         part_out[level] = gain_part
         to_owner(part_out, part_in.at[member], 2, level)
@@ -534,12 +598,12 @@
 
     @pl.when(quad > 0)
     def _():
-        remote(grad_out, grad_in, dec_send.at[1], grad_sem, section=own - 4).start()
+        remote(grad_out, grad_in, dec_send.at[1], grad_sem, **at(own - 4)).start()
 
     @pl.when(quad == 0)
     def _():
         remote(
-            grad_out, bwd_in.at[mine], dec_send.at[1], bwd_sem.at[micros + member], section=last
+            grad_out, bwd_in.at[mine], dec_send.at[1], bwd_sem.at[micros + member], **at(last)
         ).start()
 
     act_in[mine] = act_out[member]
@@ -584,7 +648,7 @@
         upstream = cube(
             (bwd_in[j].astype(F32) + scot_in[j].astype(F32)).astype(BF16).astype(F32)
         )
-        keep = keep_ref[j, own].astype(F32)
+        keep = kept_at(j, own)
         columns = spatial_taps(keep * upstream, -1)
         cot = uncube(jnp.dot(columns, enc_w[...], preferred_element_type=F32))
         grad, gain_part = norm_backward(
@@ -601,7 +665,7 @@
         def _():
             q_out[j] = flat(upstream + grad)[0]
             remote(
-                q_out.at[j], bwd_in.at[j], enc_send.at[2, j], bwd_sem.at[j], section=own - 1
+                q_out.at[j], bwd_in.at[j], enc_send.at[2, j], bwd_sem.at[j], **at(own - 1)
             ).start()
 
         dge_ref[...] += gain_part
@@ -664,7 +728,6 @@
         of = lax.rem(member + o, 4)
         wait(dec_w.at[of, half], quad_send.at[0, o])
         wait(gain_quad.at[of], quad_send.at[1, o])
-        wait(dec_w.at[of, half], half_send.at[of])
         wait(act_out.at[of], owner_send.at[0, of])
         wait(h_out.at[of], owner_send.at[1, of])
         wait(part_out.at[of], owner_send.at[2, of])
@@ -682,6 +745,14 @@
     @pl.when(quad < quads - 1)
     def _():
         wait(dec_out, dec_send.at[0])
+
+    @pl.when(odd == 1)
+    def _():
+        wait(keep_used, local_sem.at[2])
+
+        @pl.when(quad == quads - 1)
+        def _():
+            wait(noise_used, local_sem.at[4])
 
 
 def body(
@@ -708,6 +779,7 @@
         clean = jnp.where((sample_ids == clip)[:, None, None], clips[clip][None].astype(F32), clean)
     level = noise_level(timesteps)[:, None, None]
     first = (jnp.sqrt(level) * clean + jnp.sqrt(1.0 - level) * noise.astype(F32)).astype(BF16)
+    keeps = jnp.broadcast_to(keep_lists.astype(F32)[:, :, None], keep_lists.shape + (128,))
     member = np.arange(channels) // (channels // GROUPS)
     mix = jnp.asarray((member[:, None] == member[None, :]).astype(np.float32), BF16)
     vmem = pl.BlockSpec(memory_space=pltpu.VMEM)
@@ -727,11 +799,13 @@
             jax.ShapeDtypeStruct((dec_blocks, 40, channels), F32),
             jax.ShapeDtypeStruct((8, channels), F32),
         ),
-        in_specs=[pl.BlockSpec(memory_space=pltpu.SMEM), vmem, vmem, vmem, vmem, vmem, hbm, hbm],
+        in_specs=[vmem, vmem, vmem, vmem, vmem, vmem, hbm, hbm],
         out_specs=(vmem, vmem, vmem),
         scratch_shapes=[
             pltpu.VMEM((9 * channels, channels), BF16),
             pltpu.VMEM((4, 3 * channels, channels), BF16),
+            pltpu.VMEM((micros, 2 * sections, 128), F32),
+            slots(micros),
             pltpu.VMEM((4, 8, channels), F32),
             slots(micros),
             slots(micros),
@@ -760,6 +834,7 @@
             pltpu.VMEM((4, 8, channels), F32),
             pltpu.VMEM((rows, channels), BF16),
             pltpu.VMEM((rows, 3 * channels), BF16),
+            pltpu.VMEM((64, channels), F32),
             pltpu.VMEM((channels, rows), BF16),
             pltpu.VMEM((8, channels), F32),
             pltpu.VMEM((8, channels), F32),
@@ -768,7 +843,7 @@
             pltpu.VMEM((chips - 1, 8, channels), F32),
             *shares(enc_blocks),
             *shares(dec_blocks),
-            pltpu.SemaphoreType.DMA((2,)),
+            pltpu.SemaphoreType.DMA((6,)),
             pltpu.SemaphoreType.DMA((2, 4)),
             pltpu.SemaphoreType.DMA((2, 4)),
             pltpu.SemaphoreType.DMA((4,)),
@@ -794,7 +869,7 @@
             collective_id=0, has_side_effects=True, vmem_limit_bytes=60 << 20
         ),
         name="pipeline",
-    )(keep_lists, first, noise, enc_gain, dec_gain, mix, enc_weight[0], dec_weight[0])
+    )(keeps, first, noise, enc_gain, dec_gain, mix, enc_weight[0], dec_weight[0])
     part = channels // group
     gains = lax.dynamic_slice_in_dim(gains, lax.axis_index("dp") * part, part, 1)
     return (

time: 384 us -> 334 us (0.87)
  Pallas kernels: 373 us -> 318 us
    pallas_call x1, Pallas kernels: 373 us -> 318 us  [body(): pl.pallas_call(lambda *refs: pipeline_kernel(sections, micros, scale, *re...]
where the time goes in v4:
time: 334 us; the launch traced here: 330 us
  Pallas kernels  318 us (95%)
  local copies, waits for them, and re-layouts  7.14 us (2%)
  other arithmetic  4 us (1%)
    pallas_call x1, Pallas kernels, body(): pl.pallas_call(lambda *refs: pipeline_kernel(sections, micros, scale, *re...  318 us

profile of v4, /device:TPU:1, one launch (start us, length us, event | category | flops | bytes accessed | tf_op | source)
XLA Modules:
  0.0 330.0 jit_solution(173804625712003240)
XLA Ops:
  0.6 0.9 slice_convert_fusion.3
  1.7 0.7 broadcast_compare_fusion.3
  2.4 1.0 reshape.68.refs_2_
  3.4 0.0 copy-start
  3.4 0.7 fusion
  4.2 1.0 add_convert_fusion.refs_1_
  5.2 0.7 convert_element_type.56
  5.9 0.8 broadcast_in_dim.60.refs_0_
  6.7 0.0 copy-done
  6.7 318.1 %pipeline.1 = (f32[9,40,640]{2,1,0:T(8,128)}, f32[3,40,640]{2,1,0:T(8,128)}, f32[8,640]{1,0:T(8,128)}) custom-call(f32[8,32,128]{2,1,0:T(8,128)} %broadcast_in_dim.60.refs_0_, bf16[8,24,640]{2,1,0:T(8,128)(2,1)} %add_convert_fusion.refs_1_, bf16[8,24,640]{2,1,0:T(8,128)(2,1)} %copy-done, f32[1,640]{1,0:T(1,128)} %refs_3_.1, f32[1,640]{1,0:T(1,128)} %refs_4_.1, ...), custom_call_target="tpu_custom_call" | custom-call | tf_op jit(solution)/shard_map/pipeline/pallas_call | solution.py:795
  324.8 0.8 constant_dynamic-slice_fusion
  325.6 0.5 fusion.1
  326.1 2.2 copy.16
  328.2 1.7 copy.17
  (4 shorter events, 0.2 us)
Async XLA Ops:
  3.4 3.2 copy-start

commit v5 on v4

--- a/solution.py
+++ b/solution.py
@@ -123,9 +123,61 @@
     return total
 
 
-def scatter_start(p, c, sibling, dw, from_sibling, pair, from_chips, sems):
+def halving(p):
+    y, x = p // 2, lax.rem(p, 2)
+    ring = lambda row: lax.rem((row + 1) // 2, 2)
+    side, half = ring(y), y // 2
+    next_y = y + 1 - 2 * lax.rem(y, 2)
+    far_y = 3 - y
+    row = lambda which, i: which + i * (3 - 2 * which)
+    over_x, over_a, over_b = 2 * y + 1 - x, 2 * next_y + x, 2 * far_y + x
+    return [
+        dict(
+            partners=[over_x, over_a, over_b],
+            kept=[lambda i: 2 * i + x, lambda i: 2 * row(side, i) + x],
+            sent=lambda i: 2 * row(1 - side, i) + x,
+            goes=lambda m: (lax.rem(m, 2) != x, m // 2),
+        ),
+        dict(
+            partners=[over_a, over_b, over_x],
+            kept=[lambda i: 2 * row(side, i // 2) + lax.rem(i, 2), lambda i: 2 * y + i],
+            sent=lambda i: 2 * far_y + i,
+            goes=lambda m: (ring(m // 2) != side, 2 * (m // 4) + lax.rem(m, 2)),
+        ),
+        dict(
+            partners=[over_b, over_x, over_a],
+            kept=[lambda i: 4 * half + i, lambda i: 2 * (2 * half + i) + x],
+            sent=lambda i: 2 * (2 * half + i) + 1 - x,
+            goes=lambda m: (m // 4 != half, lax.rem(m, 4)),
+        ),
+    ]
+
+
+def chip_copy(c, third, src, place, buffers, sems, partner):
+    _, _, pair, from_chips = buffers
+    width = pair.shape[1] // 3
+    blocks = pl.ds(third * width, width)
+    return pltpu.make_async_remote_copy(
+        src_ref=pair.at[src, blocks],
+        dst_ref=from_chips.at[place, blocks],
+        send_sem=sems[2].at[third, place],
+        recv_sem=sems[3].at[third, place],
+        device_id={"dp": 2 * partner + c},
+        device_id_type=MESH,
+    )
+
+
+def wait_third(from_chips, third, place, sem):
+    width = from_chips.shape[1] // 3
+    ref = from_chips.at[place, pl.ds(third * width, width)]
+    pltpu.make_async_copy(ref, ref, sem.at[third, place]).wait()
+
+
+def scatter_start(p, c, sibling, buffers, sems):
+    dw, from_sibling, pair, from_chips = buffers
     chips = dw.shape[0]
-    send_pair, arrive_pair, send_chip, arrive_chip = sems
+    send_pair, arrive_pair, _, _ = sems
+    orders = halving(p)
 
     def to_sibling(o, carry):
         m = lax.rem(p + o, chips)
@@ -139,7 +191,7 @@
         ).start()
         return carry
 
-    def to_chip(o, carry):
+    def add_pair(o, carry):
         m = lax.rem(p + o, chips)
         pltpu.make_async_copy(from_sibling.at[m], from_sibling.at[m], arrive_pair.at[m]).wait()
 
@@ -150,46 +202,73 @@
             return inner
 
         lax.fori_loop(0, dw.shape[2], add, 0)
-        pltpu.make_async_remote_copy(
-            src_ref=pair.at[m],
-            dst_ref=from_chips.at[o - 1],
-            send_sem=send_chip.at[o - 1],
-            recv_sem=arrive_chip.at[o - 1],
-            device_id={"dp": 2 * m + c},
-            device_id_type=MESH,
-        ).start()
+        for third, order in enumerate(orders):
+            goes, place = order["goes"](m)
+
+            @pl.when(goes)
+            def _():
+                chip_copy(c, third, m, place, buffers, sems, order["partners"][0]).start()
+
         return carry
 
     lax.fori_loop(1, chips + 1, to_sibling, 0)
-    lax.fori_loop(1, chips, to_chip, 0)
-    pltpu.make_async_copy(from_sibling.at[p], from_sibling.at[p], arrive_pair.at[p]).wait()
-
-
-def scatter_end(p, c, dw, from_sibling, pair, from_chips, sems, out_ref):
-    chips = dw.shape[0]
-    send_pair, arrive_pair, send_chip, arrive_chip = sems
-
-    def arrive(o, carry):
-        pltpu.make_async_copy(from_chips.at[o], from_chips.at[o], arrive_chip.at[o]).wait()
-        return carry
-
-    def add(block, carry):
-        total = dw[p, c, block].astype(F32) + from_sibling[p, block].astype(F32)
-        for o in range(chips - 1):
-            total = total + from_chips[o, block].astype(F32)
-        out_ref[block] = total
-        return carry
-
-    def sent(o, carry):
-        pltpu.make_async_copy(pair.at[o], pair.at[o], send_chip.at[o]).wait()
+    lax.fori_loop(1, chips + 1, add_pair, 0)
+
+
+def scatter_step(p, c, buffers, sems, step):
+    _, _, pair, from_chips = buffers
+    width = pair.shape[1] // 3
+    base = 4 * step
+    for third, order in enumerate(halving(p)):
+
+        def take(i, carry):
+            wait_third(from_chips, third, base + i, sems[3])
+            kept = order["kept"][step](i)
+
+            def add(n, inner):
+                block = third * width + n
+                pair[kept, block] = (
+                    pair[kept, block].astype(F32) + from_chips[base + i, block].astype(F32)
+                ).astype(BF16)
+                return inner
+
+            lax.fori_loop(0, width, add, 0)
+            return carry
+
+        lax.fori_loop(0, 4 if step == 0 else 2, take, 0)
+        if step == 0:
+            for i in range(2):
+                chip_copy(
+                    c, third, order["sent"](i), 4 + i, buffers, sems, order["partners"][1]
+                ).start()
+        else:
+            partner = order["partners"][2]
+            chip_copy(c, third, partner, 6, buffers, sems, partner).start()
+
+
+def scatter_end(p, c, buffers, sems, out_ref):
+    _, from_sibling, pair, from_chips = buffers
+    chips = pair.shape[0]
+    width = pair.shape[1] // 3
+    for third in range(3):
+        wait_third(from_chips, third, 6, sems[3])
+
+        def add(n, carry):
+            block = third * width + n
+            out_ref[block] = pair[p, block].astype(F32) + from_chips[6, block].astype(F32)
+            return carry
+
+        lax.fori_loop(0, width, add, 0)
+
+    def sent(place, carry):
+        for third in range(3):
+            wait_third(from_chips, third, place, sems[2])
         return carry
 
     def sent_pair(m, carry):
-        pltpu.make_async_copy(from_sibling.at[m], from_sibling.at[m], send_pair.at[m]).wait()
-        return carry
-
-    lax.fori_loop(0, chips - 1, arrive, 0)
-    lax.fori_loop(0, dw.shape[2], add, 0)
+        pltpu.make_async_copy(from_sibling.at[m], from_sibling.at[m], sems[0].at[m]).wait()
+        return carry
+
     lax.fori_loop(0, chips - 1, sent, 0)
     lax.fori_loop(0, chips, sent_pair, 0)
 
@@ -306,6 +385,8 @@
     half_rows = dec_w.shape[1] // 2
     enc_sems = [enc_pair_sem.at[0], enc_pair_sem.at[1], enc_chip_sem.at[0], enc_chip_sem.at[1]]
     dec_sems = [dec_pair_sem.at[0], dec_pair_sem.at[1], dec_chip_sem.at[0], dec_chip_sem.at[1]]
+    enc_bufs = [enc_dw, enc_sibling, enc_pair, enc_chips]
+    dec_bufs = [dec_dw, dec_sibling, dec_pair, dec_chips]
 
     def remote(src, dst, send_sem, recv_sem, **device):
         return pltpu.make_async_remote_copy(
@@ -628,7 +709,7 @@
 
     lax.fori_loop(0, micros, lay_out, 0)
     weight_terms(dec_act[...].astype(F32).T.astype(BF16), dec_cot, dec_dw, channels)
-    scatter_start(p, c, sibling, dec_dw, dec_sibling, dec_pair, dec_chips, dec_sems)
+    scatter_start(p, c, sibling, dec_bufs, dec_sems)
 
     def enc_backward(j, carry):
         @pl.when(lax.rem(j, 2) == 0)
@@ -685,7 +766,7 @@
     )
     to_pair.start()
     weight_terms(turned[...], enc_cot, enc_dw, channels)
-    scatter_start(p, c, sibling, enc_dw, enc_sibling, enc_pair, enc_chips, enc_sems)
+    scatter_start(p, c, sibling, enc_bufs, enc_sems)
     to_pair.wait()
     gain_pair[...] = gain_own[...] + gain_sibling[...]
 
@@ -700,8 +781,11 @@
         return carry
 
     lax.fori_loop(1, chips, gain_to_chip, 0)
-    scatter_end(p, c, dec_dw, dec_sibling, dec_pair, dec_chips, dec_sems, dwd_out)
-    scatter_end(p, c, enc_dw, enc_sibling, enc_pair, enc_chips, enc_sems, dwe_out)
+    for step in range(2):
+        scatter_step(p, c, dec_bufs, dec_sems, step)
+        scatter_step(p, c, enc_bufs, enc_sems, step)
+    scatter_end(p, c, dec_bufs, dec_sems, dwd_out)
+    scatter_end(p, c, enc_bufs, enc_sems, dwe_out)
 
     def gain_arrived(o, carry):
         for side in range(2):
@@ -859,9 +943,9 @@
             pltpu.SemaphoreType.DMA((3, micros)),
             pltpu.SemaphoreType.DMA((6,)),
             pltpu.SemaphoreType.DMA((2, chips)),
-            pltpu.SemaphoreType.DMA((2, chips - 1)),
+            pltpu.SemaphoreType.DMA((2, 3, chips - 1)),
             pltpu.SemaphoreType.DMA((2, chips)),
-            pltpu.SemaphoreType.DMA((2, chips - 1)),
+            pltpu.SemaphoreType.DMA((2, 3, chips - 1)),
             pltpu.SemaphoreType.DMA((2,)),
             pltpu.SemaphoreType.DMA((2, chips - 1)),
         ],

time: 334 us -> 321 us (0.961); the launches traced: 330 us -> 321 us
  Pallas kernels: 318 us -> 309 us
    pallas_call x1, Pallas kernels: 318 us -> 309 us  [body(): pl.pallas_call(lambda *refs: pipeline_kernel(sections, micros, scale, *re...]
where the time goes in v5:
time: 321 us
  Pallas kernels  309 us (96%)
  local copies, waits for them, and re-layouts  7.14 us (2%)
  other arithmetic  4 us (1%)
    pallas_call x1, Pallas kernels, body(): pl.pallas_call(lambda *refs: pipeline_kernel(sections, micros, scale, *re...  309 us

profile of v5, /device:TPU:1, one launch (start us, length us, event | category | flops | bytes accessed | tf_op | source)
XLA Modules:
  0.0 321.1 jit_solution(522961074473841865)
XLA Ops:
  0.6 0.9 slice_convert_fusion.3
  1.7 0.7 broadcast_compare_fusion.3
  2.4 1.0 reshape.68.refs_2_
  3.4 0.0 copy-start
  3.4 0.7 fusion
  4.2 1.0 add_convert_fusion.refs_1_
  5.2 0.7 convert_element_type.56
  5.9 0.8 broadcast_in_dim.60.refs_0_
  6.7 0.0 copy-done
  6.7 309.2 %pipeline.1 = (f32[9,40,640]{2,1,0:T(8,128)}, f32[3,40,640]{2,1,0:T(8,128)}, f32[8,640]{1,0:T(8,128)}) custom-call(f32[8,32,128]{2,1,0:T(8,128)} %broadcast_in_dim.60.refs_0_, bf16[8,24,640]{2,1,0:T(8,128)(2,1)} %add_convert_fusion.refs_1_, bf16[8,24,640]{2,1,0:T(8,128)(2,1)} %copy-done, f32[1,640]{1,0:T(1,128)} %refs_3_.1, f32[1,640]{1,0:T(1,128)} %refs_4_.1, ...), custom_call_target="tpu_custom_call" | custom-call | tf_op jit(solution)/shard_map/pipeline/pallas_call | solution.py:879
  315.9 0.8 constant_dynamic-slice_fusion
  316.7 0.5 fusion.1
  317.2 2.2 copy.16
  319.4 1.7 copy.17
  (4 shorter events, 0.2 us)
Async XLA Ops:
  3.4 3.2 %copy-start = (bf16[8,24,640]{2,1,0:T(8,128)(2,1)}, bf16[8,24,640]{2,1,0:T(8,128)(2,1)S(1)}, u32[]{:S(2)}) copy-start(bf16[8,24,640]{2,1,0:T(8,128)(2,1)S(1)} %reshape.68.refs_2_) | copy-start | bytes 737284

commit v6 on v5

--- a/solution.py
+++ b/solution.py
@@ -173,26 +173,13 @@
     pltpu.make_async_copy(ref, ref, sem.at[third, place]).wait()
 
 
-def scatter_start(p, c, sibling, buffers, sems):
+def scatter_start(p, c, buffers, sems):
     dw, from_sibling, pair, from_chips = buffers
     chips = dw.shape[0]
-    send_pair, arrive_pair, _, _ = sems
+    arrive_pair = sems[1]
     orders = halving(p)
 
-    def to_sibling(o, carry):
-        m = lax.rem(p + o, chips)
-        pltpu.make_async_remote_copy(
-            src_ref=dw.at[m, 1 - c],
-            dst_ref=from_sibling.at[m],
-            send_sem=send_pair.at[m],
-            recv_sem=arrive_pair.at[m],
-            device_id={"dp": sibling},
-            device_id_type=MESH,
-        ).start()
-        return carry
-
-    def add_pair(o, carry):
-        m = lax.rem(p + o, chips)
+    def add_pair(m, carry):
         pltpu.make_async_copy(from_sibling.at[m], from_sibling.at[m], arrive_pair.at[m]).wait()
 
         def add(block, inner):
@@ -211,8 +198,7 @@
 
         return carry
 
-    lax.fori_loop(1, chips + 1, to_sibling, 0)
-    lax.fori_loop(1, chips + 1, add_pair, 0)
+    lax.fori_loop(0, chips, add_pair, 0)
 
 
 def scatter_step(p, c, buffers, sems, step):
@@ -273,17 +259,35 @@
     lax.fori_loop(0, chips, sent_pair, 0)
 
 
-def weight_terms(turned, cot, dw, channels):
+def weight_terms(turned, cot, c, sibling, buffers, sems, channels):
+    dw, from_sibling, _, _ = buffers
     blocks = dw.shape[2]
+    per_tap = channels // 40
+    gone = 0
     for tap in range(cot.shape[1] // channels):
         part = jnp.dot(
             turned,
             cot[:, tap * channels : (tap + 1) * channels],
             preferred_element_type=F32,
-        ).reshape(channels // 40, 40, channels)
-        for i in range(channels // 40):
-            at = tap * (channels // 40) + i
+        ).reshape(per_tap, 40, channels)
+        for i in range(per_tap):
+            at = tap * per_tap + i
             dw[at // (2 * blocks), (at // blocks) % 2, at % blocks] = part[i].astype(BF16)
+        ready = (tap + 1) * per_tap // (2 * blocks)
+
+        def to_sibling(m, carry):
+            pltpu.make_async_remote_copy(
+                src_ref=dw.at[m, 1 - c],
+                dst_ref=from_sibling.at[m],
+                send_sem=sems[0].at[m],
+                recv_sem=sems[1].at[m],
+                device_id={"dp": sibling},
+                device_id_type=MESH,
+            ).start()
+            return carry
+
+        lax.fori_loop(gone, ready, to_sibling, 0)
+        gone = ready
 
 
 def pipeline_kernel(
@@ -485,7 +489,6 @@
         lax.fori_loop(1, 4, share, 0)
 
     dge_ref[...] = jnp.zeros_like(dge_ref)
-    load_enc.wait()
 
     opposite = last - own
     opposite_quad, opposite_level = opposite // 4, lax.rem(opposite, 4)
@@ -500,6 +503,11 @@
         normed, scale, z, gate = norm_forward(values, enc_gain_ref[...], mix_ref, count)
         act = z * gate
         columns = spatial_taps(act, 1)
+
+        @pl.when(j == 0)
+        def _():
+            load_enc.wait()
+
         branch = uncube(jnp.dot(columns, enc_w[...], preferred_element_type=F32))
         enc_out[j] = flat(values + keep * branch)[0]
 
@@ -555,10 +563,10 @@
         wait(dec_w.at[of, other_half], half_sem.at[of])
         return carry
 
+    lax.fori_loop(0, 9, turn_tap, 0)
+    turned[...] = enc_act[...].astype(F32).T.astype(BF16)
     load_dec.wait()
     lax.fori_loop(1, 4, pass_half, 0)
-    lax.fori_loop(0, 9, turn_tap, 0)
-    turned[...] = enc_act[...].astype(F32).T.astype(BF16)
     lax.fori_loop(1, 4, take_half, 0)
 
     mine = pl.ds(2 * member, 2)
@@ -603,7 +611,6 @@
         dec_scale[level] = scale
         dec_slope[level] = gate * (1.0 + z * (1.0 - gate))
         act_out[level] = flat(act)
-        to_owner(act_out, act_in.at[mine], 0, level)
         return result
 
     result = lax.fori_loop(0, 4, dec_forward, cube(dec_in[...].astype(F32)))
@@ -641,7 +648,6 @@
         level = 3 - step
         gate = gated(upstream, dec_keeps(level))
         h_out[level] = flat(gate)
-        to_owner(h_out, h_in.at[mine], 1, level)
         columns = temporal_taps(gate, -1)
 
         @pl.when(quad < quads - 1)
@@ -663,6 +669,24 @@
             count,
         )
         s_out[level] = flat(grad)
+        part_out[level] = gain_part
+        return (upstream + grad).astype(BF16).astype(F32)
+
+    result = lax.fori_loop(0, 4, dec_backward, cube(grad_in[...].astype(F32)))
+    grad_out[...] = flat(result)
+
+    @pl.when(quad > 0)
+    def _():
+        remote(grad_out, grad_in, dec_send.at[1], grad_sem, **at(own - 4)).start()
+
+    @pl.when(quad == 0)
+    def _():
+        remote(
+            grad_out, bwd_in.at[mine], dec_send.at[1], bwd_sem.at[micros + member], **at(last)
+        ).start()
+
+    def hand_over(step, carry):
+        level = 3 - step
         remote(
             s_out.at[level],
             scot_in.at[mine],
@@ -670,22 +694,12 @@
             scot_sem.at[member],
             **at(last - 4 * quad - level),
         ).start()
-        part_out[level] = gain_part
+        to_owner(act_out, act_in.at[mine], 0, level)
+        to_owner(h_out, h_in.at[mine], 1, level)
         to_owner(part_out, part_in.at[member], 2, level)
-        return (upstream + grad).astype(BF16).astype(F32)
-
-    result = lax.fori_loop(0, 4, dec_backward, cube(grad_in[...].astype(F32)))
-    grad_out[...] = flat(result)
-
-    @pl.when(quad > 0)
-    def _():
-        remote(grad_out, grad_in, dec_send.at[1], grad_sem, **at(own - 4)).start()
-
-    @pl.when(quad == 0)
-    def _():
-        remote(
-            grad_out, bwd_in.at[mine], dec_send.at[1], bwd_sem.at[micros + member], **at(last)
-        ).start()
+        return carry
+
+    lax.fori_loop(0, 4, hand_over, 0)
 
     act_in[mine] = act_out[member]
     h_in[mine] = h_out[member]
@@ -708,8 +722,10 @@
         return carry
 
     lax.fori_loop(0, micros, lay_out, 0)
-    weight_terms(dec_act[...].astype(F32).T.astype(BF16), dec_cot, dec_dw, channels)
-    scatter_start(p, c, sibling, dec_bufs, dec_sems)
+    weight_terms(
+        dec_act[...].astype(F32).T.astype(BF16), dec_cot, c, sibling, dec_bufs, dec_sems, channels
+    )
+    scatter_start(p, c, dec_bufs, dec_sems)
 
     def enc_backward(j, carry):
         @pl.when(lax.rem(j, 2) == 0)
@@ -765,8 +781,8 @@
         gain_own, gain_sibling, gain_pair_sem.at[0], gain_pair_sem.at[1], dp=sibling
     )
     to_pair.start()
-    weight_terms(turned[...], enc_cot, enc_dw, channels)
-    scatter_start(p, c, sibling, enc_bufs, enc_sems)
+    weight_terms(turned[...], enc_cot, c, sibling, enc_bufs, enc_sems, channels)
+    scatter_start(p, c, enc_bufs, enc_sems)
     to_pair.wait()
     gain_pair[...] = gain_own[...] + gain_sibling[...]
 

time: 321 us -> 317 us (0.988)
  Pallas kernels: 309 us -> 304 us
    pallas_call x1, Pallas kernels: 309 us -> 304 us  [body(): pl.pallas_call(lambda *refs: pipeline_kernel(sections, micros, scale, *re...]
where the time goes in v6:
time: 317 us; the launch traced here: 316 us
  Pallas kernels  304 us (96%)
  local copies, waits for them, and re-layouts  7.14 us (2%)
  other arithmetic  4 us (1%)
    pallas_call x1, Pallas kernels, body(): pl.pallas_call(lambda *refs: pipeline_kernel(sections, micros, scale, *re...  304 us

profile of v6, /device:TPU:1, one launch (start us, length us, event | category | flops | bytes accessed | tf_op | source)
XLA Modules:
  0.0 315.7 jit_solution(9390698734269649439)
XLA Ops:
  0.6 0.9 slice_convert_fusion.3
  1.7 0.7 broadcast_compare_fusion.3
  2.4 1.0 reshape.68.refs_2_
  3.4 0.0 copy-start
  3.4 0.7 fusion
  4.2 1.0 add_convert_fusion.refs_1_
  5.2 0.7 convert_element_type.56
  5.9 0.8 broadcast_in_dim.60.refs_0_
  6.7 0.0 copy-done
  6.7 303.9 %pipeline.1 = (f32[9,40,640]{2,1,0:T(8,128)}, f32[3,40,640]{2,1,0:T(8,128)}, f32[8,640]{1,0:T(8,128)}) custom-call(f32[8,32,128]{2,1,0:T(8,128)} %broadcast_in_dim.60.refs_0_, bf16[8,24,640]{2,1,0:T(8,128)(2,1)} %add_convert_fusion.refs_1_, bf16[8,24,640]{2,1,0:T(8,128)(2,1)} %copy-done, f32[1,640]{1,0:T(1,128)} %refs_3_.1, f32[1,640]{1,0:T(1,128)} %refs_4_.1, ...), custom_call_target="tpu_custom_call" | custom-call | tf_op jit(solution)/shard_map/pipeline/pallas_call | solution.py:895
  310.6 0.8 constant_dynamic-slice_fusion
  311.3 0.5 fusion.1
  311.9 2.2 copy.16
  314.0 1.7 copy.17
  (4 shorter events, 0.2 us)
Async XLA Ops:
  3.4 3.2 %copy-start = (bf16[8,24,640]{2,1,0:T(8,128)(2,1)}, bf16[8,24,640]{2,1,0:T(8,128)(2,1)S(1)}, u32[]{:S(2)}) copy-start(bf16[8,24,640]{2,1,0:T(8,128)(2,1)S(1)} %reshape.68.refs_2_) | copy-start | bytes 737284
